TPU v7x, 128 devices: a whole 4x4x4 slice. The times are simulated.
128 devices in a mesh: dp: 16 (over z, y), mp: 8 (over x, core).
Axes of the slice: x: 4, y: 4, z: 4, core: 2. Of those that a mesh axis runs over, the one named last changes fastest.
Arguments:
- tokens: bfloat16 [32768, 1536], P(('dp', 'mp')), may hold values from -6 to 6
- lengths: int32 [16, 4], P('dp'), may hold values from 1 to 1024, 2048 in all within a row
- request_adapter: int32 [16, 4], P('dp'), may hold values from 0 to 15
- group_page_slots: int32 [16, 16], P('dp'), may hold values from 0 to 15, as said below
- routes: int32 [32768, 4], P(('dp', 'mp')), may hold values from 0 to 31, all different within a row; in each aligned block of 256 rows (0 to 255, 256 to 511, ...) at most 48 rows name the same one
- attention_gain: float32 [1536], replicated, may hold values from 0.1 to 1.9
- query_key_value_weight: bfloat16 [1536, 2048], P(None, 'mp')
- adapter_down_weight: bfloat16 [16, 1536, 16], P('dp'), may hold values from -0.15625 to 0.15625
- adapter_up_weight: bfloat16 [16, 16, 1536], P('dp'), may hold values from -0.75 to 0.75
- output_weight: bfloat16 [1536, 1536], P(None, 'mp'), may hold values from -0.15625 to 0.15625
- expert_norm_gain: float32 [1536], replicated, may hold values from 0.1 to 1.9
- router: bfloat16 [1536, 32], replicated, may hold values from -0.3125 to 0.3125
- expert_gate_up_weight: bfloat16 [32, 1536, 1536], P('dp'), may hold values from -0.15625 to 0.15625
- expert_down_weight: bfloat16 [32, 768, 1536], P('dp'), may hold values from -0.21875 to 0.21875
Outputs:
- layer_out: bfloat16 [32768, 1536], P(('dp', 'mp'))
- kv_pool: bfloat16 [256, 128, 512], P(('dp', 'mp'))
Inputs may be any that keep to these rules, and one draw needn't show every extreme that they name: `lengths`: each row sums to 2048, and its longest length is exactly half of 2048. `group_page_slots`: each row is a permutation of the 16 slots of its group. `routes`: A token names 4 different experts; among the rows of one device no expert is named more than 48 times.
All inputs are finite; a program needn't handle non-finite values.
Results may differ from a plain program's by a relative error of at most 0.02.
The roundings to bfloat16 on the way count: a program that leaves them out, or rounds other values in their place, can miss the bound.
Values may be sent and summed in bfloat16 or wider, within the bound.
A program may use at most 128 MiB of HBM per device.

v0:
```python
import jax
import jax.numpy as jnp
from jax import lax
from jax.sharding import PartitionSpec as P

HEAD_SIZE = 128
PAGE = 128
CAP = 48


eps = 1e-06
neg_fill = -1e30


def rms_norm(values, gains):
    widened = values.astype(jnp.float32)
    inv_rms = lax.rsqrt(jnp.mean(widened * widened, axis=-1, keepdims=True) + eps)
    return (widened * inv_rms * gains).astype(jnp.bfloat16)


def segment_ids(length_row, offset, count):
    seq_ends = jnp.cumsum(length_row)
    positions = offset + jnp.arange(count, dtype=jnp.int32)
    return jnp.sum((positions[:, None] >= seq_ends[None, :]).astype(jnp.int32), axis=1)


def shards(
    tokens,
    lengths,
    request_adapter,
    group_page_slots,
    routes,
    attention_gain,
    query_key_value_weight,
    adapter_down_weight,
    adapter_up_weight,
    output_weight,
    expert_norm_gain,
    router,
    expert_gate_up_weight,
    expert_down_weight,
):
    adapter_down_map, adapter_up_map = (
        lax.all_gather(adapter_down_weight, "dp", axis=0, tiled=True),
        lax.all_gather(adapter_up_weight, "dp", axis=0, tiled=True),
    )
    tokens_per_shard = tokens.shape[0]
    model_columns = tokens.shape[1]
    mp_index = lax.axis_index("mp")
    group_start = mp_index * tokens_per_shard
    length_row = lengths[0]
    query_seg = segment_ids(length_row, group_start, tokens_per_shard)
    normalized_input = rms_norm(tokens, attention_gain)
    full_qkv, full_out = (
        lax.all_gather(query_key_value_weight, "mp", axis=1, tiled=True),
        lax.all_gather(output_weight, "mp", axis=1, tiled=True),
    )
    complete_query_key_value = jnp.dot(
        normalized_input, full_qkv, preferred_element_type=jnp.float32
    )
    seq_count = lengths.shape[1]
    seq_match = (query_seg[:, None] == jnp.arange(seq_count, dtype=jnp.int32)[None, :]).astype(
        jnp.int32
    )
    token_adapter = jnp.sum(seq_match * request_adapter[0][None, :], axis=1)
    adapter_total = adapter_down_map.shape[0]
    adapter_rank_size = adapter_down_map.shape[2]
    query_width = adapter_up_map.shape[2]
    flattened_down = jnp.transpose(adapter_down_map, (1, 0, 2)).reshape(
        model_columns, adapter_total * adapter_rank_size
    )
    adapter_middle = jnp.dot(
        normalized_input, flattened_down, preferred_element_type=jnp.float32
    ).reshape(tokens_per_shard, adapter_total, adapter_rank_size)
    adapter_selected = token_adapter[:, None] == jnp.arange(adapter_total, dtype=jnp.int32)[None, :]
    adapter_middle = (
        jnp.where(adapter_selected[:, :, None], adapter_middle, 0.0)
        .astype(jnp.bfloat16)
        .reshape(tokens_per_shard, adapter_total * adapter_rank_size)
    )
    adapter_query = jnp.dot(
        adapter_middle,
        adapter_up_map.reshape(adapter_total * adapter_rank_size, query_width),
        preferred_element_type=jnp.float32,
    )
    query_rows = (complete_query_key_value[:, :query_width] + adapter_query).astype(jnp.bfloat16)
    key_value = complete_query_key_value[:, query_width:].astype(jnp.bfloat16)
    kv_dim = key_value.shape[1] // 2
    group_kv = lax.all_gather(key_value, "mp", axis=0, tiled=True)
    group_len = group_kv.shape[0]
    key_seg = segment_ids(length_row, 0, group_len)
    key_pos = jnp.arange(group_len, dtype=jnp.int32)
    query_pos = group_start + jnp.arange(tokens_per_shard, dtype=jnp.int32)
    allowed = (query_seg[:, None] == key_seg[None, :]) & (key_pos[None, :] <= query_pos[:, None])
    n_kv = kv_dim // HEAD_SIZE
    group_share = query_width // kv_dim
    pieces = []
    for head_position in range(n_kv):
        lo_col = head_position * group_share * HEAD_SIZE
        q_head = query_rows[:, lo_col : lo_col + group_share * HEAD_SIZE].reshape(
            tokens_per_shard, group_share, HEAD_SIZE
        )
        k_head = group_kv[:, head_position * HEAD_SIZE : (head_position + 1) * HEAD_SIZE]
        v_head = group_kv[
            :, kv_dim + head_position * HEAD_SIZE : kv_dim + (head_position + 1) * HEAD_SIZE
        ]
        scores = jnp.einsum(
            "tgd,sd->tgs", q_head, k_head, preferred_element_type=jnp.float32
        ) * HEAD_SIZE ** (-0.5)
        scores = jnp.where(allowed[:, None, :], scores, neg_fill)
        row_max = jnp.max(scores, axis=2, keepdims=True)
        expd = jnp.exp(scores - row_max)
        probs = (expd / jnp.sum(expd, axis=2, keepdims=True)).astype(jnp.bfloat16)
        mixed = jnp.einsum("tgs,sd->tgd", probs, v_head, preferred_element_type=jnp.float32)
        pieces.append(mixed.astype(jnp.bfloat16).reshape(tokens_per_shard, group_share * HEAD_SIZE))
    attended = jnp.concatenate(pieces, axis=1)
    projected = jnp.dot(attended, full_out, preferred_element_type=jnp.float32)
    residual = (tokens.astype(jnp.float32) + projected).astype(jnp.bfloat16)
    pages_dev = tokens_per_shard // PAGE
    pages_grp = group_page_slots.shape[1]
    my_slots = mp_index * pages_dev + jnp.arange(pages_dev, dtype=jnp.int32)
    slot_match = (group_page_slots[0][None, :] == my_slots[:, None]).astype(jnp.int32)
    source_page = jnp.sum(slot_match * jnp.arange(pages_grp, dtype=jnp.int32)[None, :], axis=1)
    pool = group_kv.reshape(pages_grp, PAGE, 2 * kv_dim)[source_page]
    ffn_in = rms_norm(residual, expert_norm_gain)
    logits = jnp.dot(ffn_in, router, preferred_element_type=jnp.float32)
    chosen = jnp.take_along_axis(logits, routes, axis=1)
    route_weights = jax.nn.softmax(chosen, axis=1)
    n_exp = router.shape[1]
    top_k = routes.shape[1]
    pair_expert = routes.reshape(-1)
    expert_hits = (pair_expert[:, None] == jnp.arange(n_exp, dtype=jnp.int32)[None, :]).astype(
        jnp.int32
    )
    slot_index = jnp.sum((jnp.cumsum(expert_hits, axis=0) - 1) * expert_hits, axis=1)
    target = pair_expert * CAP + slot_index
    send_rows = (
        jnp.zeros((n_exp * CAP, model_columns), jnp.bfloat16)
        .at[target]
        .set(jnp.repeat(ffn_in, top_k, axis=0))
    )
    n_dp = lax.axis_size("dp")
    exp_local = n_exp // n_dp
    outgoing = send_rows.reshape(n_dp, exp_local, CAP, model_columns)
    arrived = lax.all_to_all(outgoing, "dp", split_axis=0, concat_axis=0, tiled=True)
    gate_up = jnp.einsum(
        "secd,edf->secf", arrived, expert_gate_up_weight, preferred_element_type=jnp.float32
    )
    hidden_units = expert_down_weight.shape[1]
    active = (jnp.maximum(gate_up[..., :hidden_units], 0.0) * gate_up[..., hidden_units:]).astype(
        jnp.bfloat16
    )
    produced = jnp.einsum(
        "secf,efd->secd", active, expert_down_weight, preferred_element_type=jnp.float32
    ).astype(jnp.bfloat16)
    returned = lax.all_to_all(produced, "dp", split_axis=0, concat_axis=0, tiled=True)
    pair_out = (
        returned.reshape(n_exp * CAP, model_columns)[target]
        .astype(jnp.float32)
        .reshape(tokens_per_shard, top_k, model_columns)
    )
    mixture = jnp.sum(pair_out * route_weights[:, :, None], axis=1)
    layer_out = (residual.astype(jnp.float32) + mixture).astype(jnp.bfloat16)
    return (layer_out, pool)


def solution(mesh):
    return jax.shard_map(
        shards,
        mesh=mesh,
        in_specs=(
            P(("dp", "mp"), None),
            P("dp", None),
            P("dp", None),
            P("dp", None),
            P(("dp", "mp"), None),
            P(),
            P(None, "mp"),
            P("dp", None, None),
            P("dp", None, None),
            P(None, "mp"),
            P(),
            P(),
            P("dp", None, None),
            P("dp", None, None),
        ),
        out_specs=(P(("dp", "mp"), None), P(("dp", "mp"), None, None)),
        check_vma=False,
    )
```

profile of v0, /device:TPU:6, one launch (start us, length us, event | category | flops | bytes accessed | tf_op | source)
XLA Modules:
  0.0 358.5 jit_solution(10791619385420463547)
XLA Ops:
  9.4 46.9 %all-gather.4.cloned.1.call-done = bf16[1536,2048]{1,0:T(8,128)(2,1)} async-done(((bf16[1536,256]{1,0:T(8,128)(2,1)}), bf16[1536,2048]{1,0:T(8,128)(2,1)}) %all-gather.4.cloned.1.call-update) | async-done | bytes 6291472 | tf_op jit(solution)/shard_map/all_gather | solution.py:55
  56.3 4.9 %fusion.49 = f32[256,2048]{1,0:T(8,128)S(1)} fusion(bf16[1536,2048]{1,0:T(8,128)(2,1)} %all-gather.4.cloned.1.call-done, bf16[256,1536]{1,0:T(8,128)(2,1)} %param.14, f32[1536]{0:T(1024)} %param.19, f32[256]{0:T(256)S(1)} %add_rsqrt_fusion.1), kind=kOutput, calls=%fused_computation.68 | convolution fusion | flops 1612185600 | bytes 9182208 | tf_op jit(solution)/shard_map/dot_general | solution.py:58
  65.0 25.1 %all_gather.16 = bf16[16,1536,16]{1,2,0:T(8,128)(2,1)S(1)} all-gather(bf16[1,1536,16]{1,2,0:T(8,128)(2,1)S(1)} %copy-done.9), channel_id=1, replica_groups=mesh['dp'=16,'mp'=8] {'dp'}, dimensions={0}, use_global_device_ids=true | all-gather | bytes 835584 | tf_op jit(solution)/shard_map/all_gather | solution.py:44
  90.1 9.0 %reduce-window.19 = s32[32,8,128]{2,1,0:T(8,128)S(1)} reduce-window(s32[32,8,128]{2,1,0:T(8,128)S(1)} %fusion.54, s32[]{:T(128)} %constant.20.clone.1), window={size=1x1x128 pad=0_0x0_0x127_0}, to_apply=%region_9.10 | reduce-window | flops 4161536 | bytes 262148 | tf_op jit(solution)/shard_map/reduce-window.1
  99.9 23.2 %all_gather.17 = bf16[16,16,1536]{2,1,0:T(8,128)(2,1)S(1)} all-gather(bf16[1,16,1536]{2,1,0:T(8,128)(2,1)S(1)} %copy-done.10), channel_id=1, replica_groups=mesh['dp'=16,'mp'=8] {'dp'}, dimensions={0}, use_global_device_ids=true | all-gather | bytes 835584 | tf_op jit(solution)/shard_map/all_gather | solution.py:45
  125.3 2.6 fusion.26
  128.4 7.3 %fusion.46 = f32[256,6,2048]{2,0,1:T(8,128)} fusion(bf16[256,6,128]{0,2,1:T(8,128)(2,1)S(1)} %bitcast.93, bf16[2048,512]{1,0:T(8,128)(2,1)} %all-gather.6.cloned.1.call-done), kind=kOutput, calls=%fused_computation.66 | convolution fusion | flops 805306368 | bytes 13500416 | tf_op jit(solution)/shard_map/tgd,sd->tgs/dot_general | solution.py:107
  135.7 2.9 fusion.45
  138.6 17.6 %fusion.70 = (f32[256,6]{0,1:T(8,128)S(1)}, f32[256,6,2048]{2,0,1:T(8,128)}) fusion(f32[256,6,2048]{2,0,1:T(8,128)} %fusion.46, pred[256,2048]{1,0:T(8,128)(4,1)} %fusion.31), kind=kOutput, calls=%fused_computation.112 | output fusion | flops 18876416 | bytes 25696256 | tf_op jit(solution)/shard_map/sub | solution.py:112
  156.2 9.5 %fusion.69 = (f32[256,6]{0,1:T(8,128)S(1)}, f32[256,6,2048]{2,0,1:T(8,128)}) fusion(f32[256,6,2048]{2,0,1:T(8,128)S(1)} %fusion.45, pred[256,2048]{1,0:T(8,128)(4,1)} %fusion.31), kind=kOutput, calls=%fused_computation.111 | output fusion | flops 18876416 | bytes 25696256 | tf_op jit(solution)/shard_map/sub | solution.py:112
  165.7 7.0 %fusion.36 = bf16[256,6,128]{0,2,1:T(8,128)(2,1)S(1)} fusion(f32[256,6,2048]{2,0,1:T(8,128)} %get-tuple-element.9, f32[256,6]{0,1:T(8,128)S(1)} %get-tuple-element.8, bf16[2048,512]{1,0:T(8,128)(2,1)} %all-gather.6.cloned.1.call-done), kind=kOutput, calls=%fused_computation.53 | convolution fusion | flops 811794432 | bytes 13506560 | tf_op jit(solution)/shard_map/tgs,sd->tgd/dot_general | solution.py:114
  174.0 3.7 %fusion.35 = bf16[256,6,128]{0,2,1:T(8,128)(2,1)S(1)} fusion(f32[256,6,2048]{2,0,1:T(8,128)S(1)} %copy-done.18, f32[256,6]{0,1:T(8,128)S(1)} %get-tuple-element.6, bf16[2048,512]{1,0:T(8,128)(2,1)} %all-gather.6.cloned.1.call-done), kind=kOutput, calls=%fused_computation.52 | convolution fusion | flops 811794432 | bytes 13506560 | tf_op jit(solution)/shard_map/tgs,sd->tgd/dot_general | solution.py:114
  177.7 3.9 %multiply_reduce_fusion.1 = (f32[256]{0:T(256)S(1)}, f32[256,1536]{1,0:T(8,128)S(1)}) fusion(bf16[1536,1536]{0,1:T(8,128)(2,1)} %all-gather.8.cloned.1.call-done, bf16[256,768]{0,1:T(8,128)(2,1)S(1)} %bitcast.107, bf16[256,768]{0,1:T(8,128)(2,1)S(1)} %bitcast.106, bf16[256,1536]{1,0:T(8,128)(2,1)S(1)} %copy-done.6), kind=kOutput, calls=%fused_computation.51 | convolution fusion | flops 1211891456 | bytes 7865344 | tf_op jit(solution)/shard_map/dot_general | solution.py:117
  187.3 9.2 %scatter_custom_fusion = bf16[1536,1536]{1,0:T(8,128)(2,1)} fusion(s32[1024]{0:T(1024)S(1)} %bitcast.99, bf16[1024,1536]{1,0:T(8,128)(2,1)} %reshape.285, bf16[]{:T(256)} %constant.34.clone.1), kind=kCustom, calls=%fused_computation.42 | custom fusion | bytes 4719104 | tf_op jit(solution)/shard_map/scatter | solution.py:140
  196.5 54.8 %all_to_all.10 = bf16[16,2,48,1536]{3,2,1,0:T(8,128)(2,1)S(1)} all-to-all(bf16[16,2,48,1536]{3,2,1,0:T(8,128)(2,1)} %bitcast.92), channel_id=1, replica_groups=mesh['dp'=16,'mp'=8] {'dp'}, dimensions={0} | all-to-all | bytes 9437184 | tf_op jit(solution)/shard_map/all_to_all | solution.py:145
  251.3 10.0 %fusion.14 = f32[16,2,48,1536]{3,2,0,1:T(8,128)S(1)} fusion(bf16[2,1536,1536]{2,1,0:T(8,128)(2,1)} %param.26, bf16[16,2,48,1536]{3,2,1,0:T(8,128)(2,1)S(1)} %all_to_all.10), kind=kOutput, calls=%fused_computation.25 | convolution fusion | flops 7247757312 | bytes 23592960 | tf_op jit(solution)/shard_map/secd,edf->secf/dot_general | solution.py:146
  261.2 6.4 %convert_bitcast_fusion = bf16[16,2,48,1536]{3,2,0,1:T(8,128)(2,1)S(1)} fusion(bf16[2,768,1536]{2,1,0:T(8,128)(2,1)} %param.27, f32[16,2,48,1536]{3,2,0,1:T(8,128)S(1)} %fusion.14), kind=kOutput, calls=%fused_computation.32 | convolution fusion | flops 3629776896 | bytes 18874368 | tf_op jit(solution)/shard_map/secf,efd->secd/dot_general | solution.py:153
  270.2 4.9 %all-to-all-start.1 = ((bf16[16,2,48,1536]{3,2,1,0:T(8,128)(2,1)}), bf16[16,2,48,1536]{3,2,1,0:T(8,128)(2,1)}, u32[]{:S(2)}, u32[]{:S(2)}) async-start(bf16[16,2,48,1536]{3,2,1,0:T(8,128)(2,1)} %copy.87), calls=%async_computation.1 | async-start | bytes 9437184 | tf_op jit(solution)/shard_map/all_to_all | solution.py:156
  276.0 8.7 %gather_fusion.2 = f32[1024]{0:T(1024)S(1)} fusion(f32[256,32]{0,1:T(8,128)S(1)} %fusion.71, s32[1024]{0:T(1024)S(1)} %reshape.275), kind=kCustom, calls=%fused_computation.2 | custom fusion | bytes 16384 | tf_op jit(solution)/shard_map/jit(take_along_axis)/gather | solution.py:127
  285.1 2.9 gather_fusion.1
  288.0 41.7 %all-to-all-done.1 = bf16[16,2,48,1536]{3,2,1,0:T(8,128)(2,1)} async-done(((bf16[16,2,48,1536]{3,2,1,0:T(8,128)(2,1)}), bf16[16,2,48,1536]{3,2,1,0:T(8,128)(2,1)}, u32[]{:S(2)}, u32[]{:S(2)}) %all-to-all-start.1) | async-done | bytes 4718624 | tf_op jit(solution)/shard_map/all_to_all | solution.py:156
  329.7 9.6 %gather_fusion = bf16[1024,1536]{1,0:T(8,128)(2,1)S(1)} fusion(bf16[1536,1536]{1,0:T(8,128)(2,1)} %bitcast.28, s32[1024]{0:T(1024)S(1)} %broadcast_clamp_fusion), kind=kCustom, calls=%fused_computation | custom fusion | bytes 6295552 | tf_op jit(solution)/shard_map/gather | solution.py:158
  339.3 3.9 %reshape.258 = f32[256,4,1536]{2,1,0:T(4,128)} reshape(bf16[1024,1536]{1,0:T(8,128)(2,1)S(1)} %gather_fusion) | data formatting | bytes 9437184 | tf_op jit(solution)/shard_map/convert_element_type | solution.py:159
  343.1 7.5 %multiply_reduce_fusion = f32[256,1536]{1,0:T(8,128)S(1)} fusion(f32[256,4,1536]{2,1,0:T(4,128)} %reshape.258, f32[256,4]{1,0:T(8,128)S(1)} %copy.90), kind=kLoop, calls=%fused_computation.16 | loop fusion | flops 2752512 | bytes 7868416 | tf_op jit(solution)/shard_map/reduce_sum | solution.py:162
  (95 shorter events, 20.9 us)
Async XLA Ops:
  7.2 268.5 %copy-start = (bf16[1536,32]{0,1:T(8,128)(2,1)S(1)}, bf16[1536,32]{0,1:T(8,128)(2,1)}, u32[]{:S(2)}) copy-start(bf16[1536,32]{0,1:T(8,128)(2,1)} %param.25) | copy-start | bytes 294916
  7.2 49.2 %all-gather.4.cloned.1.call-start = ((), (), s32[]{:S(2)}) async-start(), calls=%async_computation.2 | async-start | bytes 7077888 | tf_op jit(solution)/shard_map/all_gather | solution.py:55
  7.9 120.4 %all-gather.6.cloned.1.call-start = ((), (), s32[]{:S(2)}) async-start(), calls=%async_computation.3 | async-start | bytes 2359296 | tf_op jit(solution)/shard_map/all_gather | solution.py:89
  9.3 54.8 %copy-start.7 = (s32[256,4]{0,1:T(4,128)S(1)}, s32[256,4]{0,1:T(4,128)}, u32[]{:S(2)}) copy-start(s32[256,4]{0,1:T(4,128)} %param.18) | copy-start | bytes 12292
  9.3 55.2 %copy-start.16 = (s32[1,4]{1,0:T(1,128)S(1)}, s32[1,4]{1,0:T(1,128)}, u32[]{:S(2)}) copy-start(s32[1,4]{1,0:T(1,128)} %param.15) | copy-start | bytes 52
  9.4 55.5 %copy-start.14 = (s32[1,4]{1,0:T(1,128)S(1)}, s32[1,4]{1,0:T(1,128)}, u32[]{:S(2)}) copy-start(s32[1,4]{1,0:T(1,128)} %param.16) | copy-start | bytes 52
  9.4 55.6 %copy-start.9 = (bf16[1,1536,16]{1,2,0:T(8,128)(2,1)S(1)}, bf16[1,1536,16]{1,2,0:T(8,128)(2,1)}, u32[]{:S(2)}) copy-start(bf16[1,1536,16]{1,2,0:T(8,128)(2,1)} %param.21) | copy-start | bytes 147460
  9.4 90.5 %copy-start.10 = (bf16[1,16,1536]{2,1,0:T(8,128)(2,1)S(1)}, bf16[1,16,1536]{2,1,0:T(8,128)(2,1)}, u32[]{:S(2)}) copy-start(bf16[1,16,1536]{2,1,0:T(8,128)(2,1)} %param.22) | copy-start | bytes 147460
  61.2 1.4 copy-start.11
  62.6 62.7 %copy-start.5 = (bf16[256,1536]{1,0:T(8,128)(2,1)S(1)}, bf16[256,1536]{1,0:T(8,128)(2,1)}, u32[]{:S(2)}) copy-start(bf16[256,1536]{1,0:T(8,128)(2,1)} %param.14) | copy-start | bytes 2359300
  62.6 62.7 %copy-start.15 = (f32[1536]{0:T(1024)S(1)}, f32[1536]{0:T(1024)}, u32[]{:S(2)}) copy-start(f32[1536]{0:T(1024)} %param.19) | copy-start | bytes 18436
  63.4 114.4 %all-gather.8.cloned.1.call-start = ((), (), s32[]{:S(2)}) async-start(), calls=%async_computation.4 | async-start | bytes 5308416 | tf_op jit(solution)/shard_map/all_gather | solution.py:56
  165.7 8.3 %copy-start.18 = (f32[256,6,2048]{2,0,1:T(8,128)S(1)}, f32[256,6,2048]{2,0,1:T(8,128)}, u32[]{:S(2)}) copy-start(f32[256,6,2048]{2,0,1:T(8,128)} %get-tuple-element.7) | copy-start | bytes 37748740
  174.0 3.7 %copy-start.6 = (bf16[256,1536]{1,0:T(8,128)(2,1)S(1)}, bf16[256,1536]{1,0:T(8,128)(2,1)}, u32[]{:S(2)}) copy-start(bf16[256,1536]{1,0:T(8,128)(2,1)} %param.14) | copy-start | bytes 2359300
  177.7 5.1 %copy-start.13 = (f32[1536]{0:T(1024)S(1)}, f32[1536]{0:T(1024)}, u32[]{:S(2)}) copy-start(f32[1536]{0:T(1024)} %param.24) | copy-start | bytes 18436
  181.6 1.2 copy-start.3
  183.0 0.9 copy-start.1
  183.9 3.4 copy-start.12
  270.2 4.9 %copy-start.8 = (s32[256,4]{0,1:T(4,128)S(1)}, s32[256,4]{0,1:T(4,128)}, u32[]{:S(2)}) copy-start(s32[256,4]{0,1:T(4,128)} %param.18) | copy-start | bytes 12292
  270.2 5.2 %copy-start.17 = (s32[1,16]{1,0:T(1,128)S(1)}, s32[1,16]{1,0:T(1,128)}, u32[]{:S(2)}) copy-start(s32[1,16]{1,0:T(1,128)} %param.17) | copy-start | bytes 196
  270.2 5.5 %copy-start.2 = (bf16[256,1536]{1,0:T(8,128)(2,1)S(1)}, bf16[256,1536]{1,0:T(8,128)(2,1)}, u32[]{:S(2)}) copy-start(bf16[256,1536]{1,0:T(8,128)(2,1)} %copy-done.1) | copy-start | bytes 2359300
  270.2 59.4 %all-to-all-start.1 = ((bf16[16,2,48,1536]{3,2,1,0:T(8,128)(2,1)}), bf16[16,2,48,1536]{3,2,1,0:T(8,128)(2,1)}, u32[]{:S(2)}, u32[]{:S(2)}) async-start(bf16[16,2,48,1536]{3,2,1,0:T(8,128)(2,1)} %copy.87), calls=%async_computation.1 | async-start | bytes 9437184 | tf_op jit(solution)/shard_map/all_to_all | solution.py:156
  343.1 7.5 %copy-start.4 = (f32[256,1536]{1,0:T(8,128)S(1)}, f32[256,1536]{1,0:T(8,128)}, u32[]{:S(2)}) copy-start(f32[256,1536]{1,0:T(8,128)} %copy-done.3) | copy-start | bytes 4718596
Sparse Core Ops, SparseCore 0:
  9.7 46.5 all-gather.3
  63.5 25.8 all-gather.5
  91.0 33.7 all-gather.7
where the time goes:
time: 365 us; the launch traced here: 358 us
  blocking collectives  103 us (28%)
  waiting for transfers between devices  90.1 us (25%)
  other arithmetic  49.3 us (14%)
  matrix products  49 us (13%)
  local copies, waits for them, and re-layouts  47.6 us (13%)
  between operations  14.4 us (4%)
  starting transfers between devices  5.02 us (1%)
    all_to_all x1, blocking collectives, shards(): lax.all_to_all(outgoing, 'dp', split_axis=0, concat_axis=0, tiled=True)  54.8 us
    all_gather x1, waiting for transfers between devices, shards(): lax.all_gather(query_key_value_weight, 'mp', axis=1, tiled=True)  46.9 us
    all_to_all x1, waiting for transfers between devices, shards(): lax.all_to_all(produced, 'dp', split_axis=0, concat_axis=0, tiled=True)  41.7 us
    sub x2, other arithmetic, shards(): expd = jnp.exp(scores - row_max)  27.1 us
    all_gather x1, blocking collectives, shards(): lax.all_gather(adapter_down_weight, 'dp', axis=0, tiled=True)  25.1 us
    all_gather x1, blocking collectives, shards(): lax.all_gather(adapter_up_weight, 'dp', axis=0, tiled=True)  23.2 us
    dot_general x2, matrix products, shards(): jnp.einsum('tgs,sd->tgd', probs, v_head, preferred_element_type=jnp.float32)  10.7 us
    dot_general x2, matrix products, shards(): jnp.einsum('tgd,sd->tgs', q_head, k_head, preferred_element_type=jnp.floa...  10.2 us
  transfers between devices with their start and end apart: 4, of which 2 were waited for; matrix products, arithmetic and copies ran while one was open for 22% of the time, Pallas kernels for 0%

commit v1 on v0

v1 whole, which is shorter than its diff:
```python
import functools

import jax
import jax.numpy as jnp
from jax import lax
from jax.experimental import pallas as pl
from jax.experimental.pallas import tpu as pltpu
from jax.sharding import PartitionSpec as P

HEAD_SIZE = 128
PAGE = 128
CAP = 48
SPAN = 1024

eps = 1e-06
neg_fill = -1e30


def rms_norm(values, gains):
    widened = values.astype(jnp.float32)
    inv_rms = lax.rsqrt(jnp.mean(widened * widened, axis=-1, keepdims=True) + eps)
    return (widened * inv_rms * gains).astype(jnp.bfloat16)


def attention_kernel(start_ref, low_ref, q_ref, k_ref, v_ref, o_ref, bias_ref):
    start = pl.multiple_of(start_ref[0], 256)
    window = bias_ref.shape[1]
    rows = bias_ref.shape[0]

    @pl.when(pl.program_id(0) == 0)
    def _():
        key = lax.broadcasted_iota(jnp.int32, (rows, window), 1) + start
        query = lax.broadcasted_iota(jnp.int32, (rows, window), 0) + start_ref[1]
        allowed = (key >= low_ref[...]) & (key <= query)
        bias_ref[...] = jnp.where(allowed, 0.0, neg_fill)

    keys = k_ref[pl.ds(start, window), :]
    values = v_ref[pl.ds(start, window), :]
    scores = lax.dot_general(
        q_ref[...], keys, (((1,), (1,)), ((), ())), preferred_element_type=jnp.float32
    )
    scores = scores + bias_ref[...]
    row_max = jnp.max(scores, axis=1, keepdims=True)
    expd = jnp.exp((scores - row_max) * HEAD_SIZE ** (-0.5))
    total = jnp.sum(expd, axis=1, keepdims=True)
    mixed = jnp.dot(expd.astype(jnp.bfloat16), values, preferred_element_type=jnp.float32)
    o_ref[...] = (mixed / total).astype(jnp.bfloat16)


def attend(query_rows, group_kv, low, start, first):
    rows, width = query_rows.shape
    group_len, kv_cols = group_kv.shape
    n_kv = kv_cols // 2 // HEAD_SIZE
    share = width // HEAD_SIZE // n_kv
    window = min(group_len, rows + SPAN)
    heads = width // HEAD_SIZE
    return pl.pallas_call(
        attention_kernel,
        grid_spec=pltpu.PrefetchScalarGridSpec(
            num_scalar_prefetch=1,
            grid=(heads,),
            in_specs=[
                pl.BlockSpec((rows, 1), lambda h, s: (0, 0)),
                pl.BlockSpec((rows, HEAD_SIZE), lambda h, s: (0, h)),
                pl.BlockSpec((group_len, HEAD_SIZE), lambda h, s: (0, h // share)),
                pl.BlockSpec((group_len, HEAD_SIZE), lambda h, s: (0, n_kv + h // share)),
            ],
            out_specs=pl.BlockSpec((rows, HEAD_SIZE), lambda h, s: (0, h)),
            scratch_shapes=[pltpu.VMEM((rows, window), jnp.float32)],
        ),
        out_shape=jax.ShapeDtypeStruct((rows, width), jnp.bfloat16),
        cost_estimate=pl.CostEstimate(
            flops=4 * rows * window * width, bytes_accessed=4 << 20, transcendentals=rows * window * heads
        ),
        name="attention",
    )(jnp.stack([start, first]), low, query_rows, group_kv, group_kv)


def shards(
    tokens,
    lengths,
    request_adapter,
    group_page_slots,
    routes,
    attention_gain,
    query_key_value_weight,
    adapter_down_weight,
    adapter_up_weight,
    output_weight,
    expert_norm_gain,
    router,
    expert_gate_up_weight,
    expert_down_weight,
):
    tokens_per_shard, model_columns = tokens.shape
    mp_index = lax.axis_index("mp")
    group_start = mp_index * tokens_per_shard
    n_exp = router.shape[1]

    full_qkv = lax.all_gather(query_key_value_weight, "mp", axis=1, tiled=True)
    packed = jnp.concatenate([adapter_down_weight[0].T, adapter_up_weight[0]], axis=0)
    rank = adapter_up_weight.shape[1]
    adapters = lax.all_gather(packed, "dp", axis=0, tiled=False)
    adapter_total = adapters.shape[0]
    down = adapters[:, :rank].reshape(adapter_total * rank, model_columns)
    up = adapters[:, rank:].reshape(adapter_total * rank, adapter_up_weight.shape[2])
    full_out = lax.all_gather(output_weight, "mp", axis=1, tiled=True)

    seq_ends = jnp.sum(
        jnp.where(
            jnp.arange(lengths.shape[1])[:, None] <= jnp.arange(lengths.shape[1])[None, :],
            lengths[0][:, None],
            0,
        ),
        axis=0,
    )
    positions = group_start + jnp.arange(tokens_per_shard, dtype=jnp.int32)
    passed = positions[:, None] >= seq_ends[None, :]
    query_seg = jnp.sum(passed.astype(jnp.int32), axis=1)
    low = jnp.max(jnp.where(passed, seq_ends[None, :], 0), axis=1, keepdims=True)
    seq_match = query_seg[:, None] == jnp.arange(lengths.shape[1], dtype=jnp.int32)[None, :]
    token_adapter = jnp.sum(jnp.where(seq_match, request_adapter[0][None, :], 0), axis=1)

    normed = rms_norm(tokens, attention_gain)
    qkv = jnp.dot(normed, full_qkv, preferred_element_type=jnp.float32)
    query_width = up.shape[1]
    key_value = qkv[:, query_width:].astype(jnp.bfloat16)
    group_kv = lax.all_gather(key_value, "mp", axis=0, tiled=True)

    middle = lax.dot_general(
        normed, down, (((1,), (1,)), ((), ())), preferred_element_type=jnp.float32
    )
    owner = jnp.arange(adapter_total * rank, dtype=jnp.int32) // rank
    middle = jnp.where(token_adapter[:, None] == owner[None, :], middle, 0.0).astype(jnp.bfloat16)
    adapter_query = jnp.dot(middle, up, preferred_element_type=jnp.float32)
    query_rows = (qkv[:, :query_width] + adapter_query).astype(jnp.bfloat16)

    group_len = group_kv.shape[0]
    window = min(group_len, tokens_per_shard + SPAN)
    start = jnp.maximum(group_start + tokens_per_shard - window, 0)
    attended = attend(query_rows, group_kv, low, start, group_start)
    projected = jnp.dot(attended, full_out, preferred_element_type=jnp.float32)
    residual = (tokens.astype(jnp.float32) + projected).astype(jnp.bfloat16)

    pages_dev = tokens_per_shard // PAGE
    pages_grp = group_page_slots.shape[1]
    my_slots = mp_index * pages_dev + jnp.arange(pages_dev, dtype=jnp.int32)
    slot_match = (group_page_slots[0][None, :] == my_slots[:, None]).astype(jnp.int32)
    source_page = jnp.sum(slot_match * jnp.arange(pages_grp, dtype=jnp.int32)[None, :], axis=1)
    pages = group_kv.reshape(pages_grp, PAGE, group_kv.shape[1])
    pool = jnp.concatenate(
        [lax.dynamic_slice_in_dim(pages, source_page[i], 1, axis=0) for i in range(pages_dev)], axis=0
    )

    ffn_in = rms_norm(residual, expert_norm_gain)
    logits = jnp.dot(ffn_in, router, preferred_element_type=jnp.float32)
    hits = jnp.any(routes[:, :, None] == jnp.arange(n_exp, dtype=jnp.int32)[None, None, :], axis=1)
    peak = jnp.max(jnp.where(hits, logits, neg_fill), axis=1, keepdims=True)
    expl = jnp.where(hits, jnp.exp(jnp.where(hits, logits, peak) - peak), 0.0)
    route_weights = expl / jnp.sum(expl, axis=1, keepdims=True)
    before = (
        jnp.arange(tokens_per_shard)[None, :] < jnp.arange(tokens_per_shard)[:, None]
    ).astype(jnp.bfloat16)
    place = jnp.dot(before, hits.astype(jnp.bfloat16), preferred_element_type=jnp.float32)
    place = jnp.where(hits, place, -1.0).T
    chosen = place[:, None, :] == jnp.arange(CAP, dtype=jnp.int32).astype(jnp.float32)[None, :, None]
    send_map = chosen.astype(jnp.bfloat16).reshape(n_exp * CAP, tokens_per_shard)
    send_rows = jnp.dot(send_map, ffn_in, preferred_element_type=jnp.float32).astype(jnp.bfloat16)
    high = route_weights.astype(jnp.bfloat16)
    rest = (route_weights - high.astype(jnp.float32)).astype(jnp.bfloat16)
    zero = jnp.zeros((), jnp.bfloat16)
    back_high = jnp.where(chosen, high.T[:, None, :], zero).reshape(n_exp * CAP, tokens_per_shard)
    back_rest = jnp.where(chosen, rest.T[:, None, :], zero).reshape(n_exp * CAP, tokens_per_shard)

    n_dp = lax.axis_size("dp")
    exp_local = n_exp // n_dp
    outgoing = send_rows.reshape(n_dp, exp_local, CAP, model_columns)
    arrived = lax.all_to_all(outgoing, "dp", split_axis=0, concat_axis=0, tiled=True)
    gate_up = jnp.einsum(
        "secd,edf->secf", arrived, expert_gate_up_weight, preferred_element_type=jnp.float32
    )
    hidden_units = expert_down_weight.shape[1]
    active = (jnp.maximum(gate_up[..., :hidden_units], 0.0) * gate_up[..., hidden_units:]).astype(
        jnp.bfloat16
    )
    produced = jnp.einsum(
        "secf,efd->secd", active, expert_down_weight, preferred_element_type=jnp.float32
    ).astype(jnp.bfloat16)
    returned = lax.all_to_all(produced, "dp", split_axis=0, concat_axis=0, tiled=True)
    returned = returned.reshape(n_exp * CAP, model_columns)
    first_dim = (((0,), (0,)), ((), ()))
    mixture = lax.dot_general(back_high, returned, first_dim, preferred_element_type=jnp.float32)
    mixture = mixture + lax.dot_general(back_rest, returned, first_dim, preferred_element_type=jnp.float32)
    layer_out = (residual.astype(jnp.float32) + mixture).astype(jnp.bfloat16)
    return (layer_out, pool)


def solution(mesh):
    return jax.shard_map(
        shards,
        mesh=mesh,
        in_specs=(
            P(("dp", "mp"), None),
            P("dp", None),
            P("dp", None),
            P("dp", None),
            P(("dp", "mp"), None),
            P(),
            P(None, "mp"),
            P("dp", None, None),
            P("dp", None, None),
            P(None, "mp"),
            P(),
            P(),
            P("dp", None, None),
            P("dp", None, None),
        ),
        out_specs=(P(("dp", "mp"), None), P(("dp", "mp"), None, None)),
        check_vma=False,
    )
```

time: 365 us -> 347 us (0.951); the launches traced: 358 us -> 344 us
  waiting for transfers between devices: 90.1 us -> 189 us
  other arithmetic: 49.3 us -> 5.3 us
  blocking collectives: 103 us -> 63.9 us
  local copies, waits for them, and re-layouts: 47.6 us -> 11 us
  Pallas kernels: 0 us -> 14.6 us
  matrix products: 49 us -> 38.1 us
    all_gather x2 -> x3, waiting for transfers between devices: 47 us -> 105 us  [the longest x1 45.4 us: shards(): full_qkv = lax.all_gather(query_key_value_weight, 'mp', axis=1, tiled=True)]
    all_gather x2 -> x0, blocking collectives: 48.3 us -> none  [the longest x1 25.1 us: shards(): lax.all_gather(adapter_down_weight, 'dp', axis=0, tiled=True)]
    sub x3 -> x0, other arithmetic: 27.2 us -> none  [the longest x2 27.1 us: shards(): expd = jnp.exp(scores - row_max)]
    gather x7 -> x0, local copies, waits for them, and re-layouts: 21.6 us -> none  [the longest x1 9.6 us: shards(): returned.reshape(n_exp * CAP, model_columns)[target].astype(jnp.float32)]
    all_gather x1, waiting for transfers between devices: 0.02 us -> 20.9 us  [shards(): group_kv = lax.all_gather(key_value, 'mp', axis=0, tiled=True)]
    all_to_all x1, waiting for transfers between devices: 41.7 us -> 61.7 us  [shards(): lax.all_to_all(produced, 'dp', split_axis=0, concat_axis=0, tiled=True)]
    pallas_call x0 -> x1, Pallas kernels: none -> 14.6 us  [attend(): pl.pallas_call(attention_kernel, grid_spec=pltpu.PrefetchScalarGridSpec(n...]
    dot_general x6, matrix products: 28.4 us -> 18.3 us  [the longest x1 4.89 us: shards(): qkv = jnp.dot(normed, full_qkv, preferred_element_type=jnp.float32)]
  transfers between devices with their start and end apart: 4 -> 5, of which waited for: 2 -> 5; matrix products, arithmetic and copies ran while one was open for 22% -> 5% of each run, Pallas kernels for 0% -> 4%
where the time goes in v1:
time: 347 us; the launch traced here: 344 us
  waiting for transfers between devices  189 us (54%)
  blocking collectives  63.9 us (18%)
  matrix products  38.1 us (11%)
  between operations  17.9 us (5%)
  Pallas kernels  14.6 us (4%)
  local copies, waits for them, and re-layouts  11 us (3%)
  other arithmetic  5.3 us (2%)
  starting transfers between devices  4.86 us (1%)
    all_to_all x1, blocking collectives, shards(): lax.all_to_all(outgoing, 'dp', split_axis=0, concat_axis=0, tiled=True)  63.9 us
    all_to_all x1, waiting for transfers between devices, shards(): lax.all_to_all(produced, 'dp', split_axis=0, concat_axis=0, tiled=True)  61.7 us
    all_gather x1, waiting for transfers between devices, shards(): full_qkv = lax.all_gather(query_key_value_weight, 'mp', axis=1, tiled=True)  45.4 us
    all_gather x1, waiting for transfers between devices, shards(): adapters = lax.all_gather(packed, 'dp', axis=0, tiled=False)  38.5 us
    all_gather x1, waiting for transfers between devices, shards(): group_kv = lax.all_gather(key_value, 'mp', axis=0, tiled=True)  20.9 us
    all_gather x1, waiting for transfers between devices, shards(): full_out = lax.all_gather(output_weight, 'mp', axis=1, tiled=True)  20.7 us
    pallas_call x1, Pallas kernels, attend(): pl.pallas_call(attention_kernel, grid_spec=pltpu.PrefetchScalarGridSpec(n...  14.6 us
    dot_general x1, matrix products, shards(): jnp.einsum('secf,efd->secd', active, expert_down_weight, preferred_elemen...  7.86 us
  transfers between devices with their start and end apart: 5, of which 5 were waited for; matrix products, arithmetic and copies ran while one was open for 5% of the time, Pallas kernels for 4%

profile of v1, /device:TPU:6, one launch (start us, length us, event | category | flops | bytes accessed | tf_op | source)
XLA Modules:
  0.0 344.2 jit_solution(16889289092596144759)
XLA Ops:
  8.0 1.5 pad_maximum_fusion.1
  9.5 1.4 fusion.18
  10.9 45.4 %all-gather.6.cloned.1.call-done = bf16[1536,2048]{1,0:T(8,128)(2,1)} async-done(((bf16[1536,256]{1,0:T(8,128)(2,1)}), bf16[1536,2048]{1,0:T(8,128)(2,1)}) %all-gather.6.cloned.1.call-update) | async-done | bytes 6291472 | tf_op jit(solution)/shard_map/all_gather | solution.py:100
  56.3 4.9 %fusion.25 = f32[256,2048]{1,0:T(8,128)S(1)} fusion(bf16[1536,2048]{1,0:T(8,128)(2,1)} %all-gather.6.cloned.1.call-done, bf16[256,1536]{1,0:T(8,128)(2,1)} %param.14, f32[1536]{0:T(1024)} %param.19, f32[256]{0:T(256)S(1)} %add_rsqrt_fusion.1), kind=kOutput, calls=%fused_computation.37 | convolution fusion | flops 1612185600 | bytes 9182208 | tf_op jit(solution)/shard_map/dot_general | solution.py:125
  61.2 1.4 copy-done.2
  62.6 0.7 slice.49
  64.3 0.8 copy.26.low_ref
  66.3 38.5 %all-gather.12.cloned.1.call-done = bf16[512,1536]{1,0:T(8,128)(2,1)} async-done(((bf16[32,1536]{1,0:T(8,128)(2,1)}), bf16[512,1536]{1,0:T(8,128)(2,1)}) %all-gather.12.cloned.1.call-update) | async-done | bytes 1572880 | tf_op jit(solution)/shard_map/all_gather | solution.py:103
  104.8 1.5 fusion.42
  106.3 3.3 fusion.13.q_ref
  109.6 20.9 %all-gather.8.cloned.1.call-done.k_ref.v_ref = bf16[2048,512]{1,0:T(8,128)(2,1)} async-done(((bf16[256,512]{1,0:T(8,128)(2,1)}), bf16[2048,512]{1,0:T(8,128)(2,1)}) %all-gather.8.cloned.1.call-update) | async-done | bytes 2097168 | tf_op jit(solution)/shard_map/all_gather | solution.py:128
  130.5 14.6 %attention.1 = bf16[256,1536]{1,0:T(8,128)(2,1)} custom-call(s32[2]{0:T(128)} %pad_add_fusion.start_ref, s32[256,1]{1,0:T(8,128)} %copy.26.low_ref, bf16[256,1536]{1,0:T(8,128)(2,1)} %fusion.13.q_ref, bf16[2048,512]{1,0:T(8,128)(2,1)} %all-gather.8.cloned.1.call-done.k_ref.v_ref, bf16[2048,512]{1,0:T(8,128)(2,1)} %all-gather.8.cloned.1.call-done.k_ref.v_ref), custom_call_target="tpu_custom_call" | custom-call | flops 2013265920 | bytes 4194304 | tf_op jit(solution)/shard_map/attention/pallas_call | solution.py:57
  145.1 20.7 %all-gather.10.cloned.1.call-done = bf16[1536,1536]{0,1:T(8,128)(2,1)} async-done(((bf16[1536,192]{0,1:T(8,128)(2,1)}), bf16[1536,1536]{0,1:T(8,128)(2,1)}) %all-gather.10.cloned.1.call-update) | async-done | bytes 4718608 | tf_op jit(solution)/shard_map/all_gather | solution.py:107
  165.8 4.1 %multiply_reduce_fusion = (f32[256]{0:T(256)S(1)}, f32[256,1536]{1,0:T(8,128)S(1)}) fusion(bf16[256,1536]{1,0:T(8,128)(2,1)} %attention.1, bf16[1536,1536]{0,1:T(8,128)(2,1)} %all-gather.10.cloned.1.call-done, bf16[256,1536]{1,0:T(8,128)(2,1)S(1)} %copy-done.1), kind=kOutput, calls=%fused_computation.29 | convolution fusion | flops 1210318592 | bytes 7865344 | tf_op jit(solution)/shard_map/dot_general | solution.py:142
  169.9 1.5 convolution_convert_fusion
  171.4 63.9 %all_to_all.10 = bf16[16,2,48,1536]{3,2,1,0:T(8,128)(2,1)S(1)} all-to-all(bf16[16,2,48,1536]{3,2,1,0:T(8,128)(2,1)S(1)} %bitcast.79), channel_id=1, replica_groups=mesh['dp'=16,'mp'=8] {'dp'}, dimensions={0} | all-to-all | bytes 9437184 | tf_op jit(solution)/shard_map/all_to_all | solution.py:178
  235.4 7.5 %fusion.2 = f32[16,2,48,1536]{3,2,0,1:T(8,128)S(1)} fusion(bf16[2,1536,1536]{2,1,0:T(8,128)(2,1)S(1)} %bitcast.81, bf16[16,2,48,1536]{3,2,1,0:T(8,128)(2,1)S(1)} %all_to_all.10), kind=kOutput, calls=%fused_computation.3 | convolution fusion | flops 7247757312 | bytes 23592960 | tf_op jit(solution)/shard_map/secd,edf->secf/dot_general | solution.py:179
  242.8 7.9 %convert_bitcast_fusion = bf16[16,2,48,1536]{3,2,0,1:T(8,128)(2,1)} fusion(bf16[2,768,1536]{2,1,0:T(8,128)(2,1)} %param.27, f32[16,2,48,1536]{3,2,0,1:T(8,128)S(1)} %fusion.2), kind=kOutput, calls=%fused_computation.10 | convolution fusion | flops 3629776896 | bytes 18874368 | tf_op jit(solution)/shard_map/secf,efd->secd/dot_general | solution.py:186
  250.7 4.9 %copy.28 = bf16[16,2,48,1536]{3,2,1,0:T(8,128)(2,1)} copy(bf16[16,2,48,1536]{3,2,0,1:T(8,128)(2,1)} %convert_bitcast_fusion) | data formatting | bytes 9437184 | tf_op jit(solution)/shard_map/convert_element_type | solution.py:188
  255.6 4.7 %all-to-all-start.1 = ((bf16[16,2,48,1536]{3,2,1,0:T(8,128)(2,1)}), bf16[16,2,48,1536]{3,2,1,0:T(8,128)(2,1)}, u32[]{:S(2)}, u32[]{:S(2)}) async-start(bf16[16,2,48,1536]{3,2,1,0:T(8,128)(2,1)} %copy.28), calls=%async_computation.1 | async-start | bytes 9437184 | tf_op jit(solution)/shard_map/all_to_all | solution.py:189
  265.5 1.0 constant_dynamic-slice_fusion
  267.5 61.7 %all-to-all-done.1 = bf16[16,2,48,1536]{3,2,1,0:T(8,128)(2,1)} async-done(((bf16[16,2,48,1536]{3,2,1,0:T(8,128)(2,1)}), bf16[16,2,48,1536]{3,2,1,0:T(8,128)(2,1)}, u32[]{:S(2)}, u32[]{:S(2)}) %all-to-all-start.1) | async-done | bytes 4718624 | tf_op jit(solution)/shard_map/all_to_all | solution.py:189
  329.3 3.7 %fusion.44 = f32[256,1536]{1,0:T(8,128)S(1)} fusion(bf16[1536,256]{1,0:T(8,128)(2,1)S(1)} %bitcast.86, bf16[1536,1536]{1,0:T(8,128)(2,1)} %bitcast.22), kind=kOutput, calls=%fused_computation.80 | convolution fusion | flops 1207959552 | bytes 7077888 | tf_op jit(solution)/shard_map/dot_general | solution.py:192
  333.0 4.6 %fusion.12 = bf16[256,1536]{1,0:T(8,128)(2,1)} fusion(f32[256,1536]{1,0:T(8,128)S(1)} %get-tuple-element.15, f32[256,1536]{1,0:T(8,128)S(1)} %fusion.44, bf16[1536,256]{1,0:T(8,128)(2,1)S(1)} %bitcast.85, bf16[1536,1536]{1,0:T(8,128)(2,1)} %bitcast.22), kind=kOutput, calls=%fused_computation.15 | convolution fusion | flops 1209139200 | bytes 9437184 | tf_op jit(solution)/shard_map/dot_general | solution.py:193
  (54 shorter events, 5.2 us)
Async XLA Ops:
  7.2 257.8 %copy-start = (bf16[1536,32]{0,1:T(8,128)(2,1)S(1)}, bf16[1536,32]{0,1:T(8,128)(2,1)}, u32[]{:S(2)}) copy-start(bf16[1536,32]{0,1:T(8,128)(2,1)} %param.25) | copy-start | bytes 294916
  7.2 49.2 %all-gather.6.cloned.1.call-start = ((), (), s32[]{:S(2)}) async-start(), calls=%async_computation.2 | async-start | bytes 7077888 | tf_op jit(solution)/shard_map/all_gather | solution.py:100
  7.9 96.9 %all-gather.12.cloned.1.call-start = ((), (), s32[]{:S(2)}) async-start(), calls=%async_computation.5 | async-start | bytes 1671168 | tf_op jit(solution)/shard_map/all_gather | solution.py:103
  9.5 121.1 %all-gather.8.cloned.1.call-start = ((), (), s32[]{:S(2)}) async-start(), calls=%async_computation.3 | async-start | bytes 2359296 | tf_op jit(solution)/shard_map/all_gather | solution.py:128
  10.9 53.2 %copy-start.7 = (s32[1,4]{1,0:T(1,128)S(1)}, s32[1,4]{1,0:T(1,128)}, u32[]{:S(2)}) copy-start(s32[1,4]{1,0:T(1,128)} %param.15) | copy-start | bytes 52
  10.9 54.2 %copy-start.5 = (s32[256,4]{0,1:T(4,128)S(1)}, s32[256,4]{0,1:T(4,128)}, u32[]{:S(2)}) copy-start(s32[256,4]{0,1:T(4,128)} %param.18) | copy-start | bytes 12292
  61.2 1.4 copy-start.2
  62.6 3.6 %copy-start.6 = (s32[1,4]{1,0:T(1,128)S(1)}, s32[1,4]{1,0:T(1,128)}, u32[]{:S(2)}) copy-start(s32[1,4]{1,0:T(1,128)} %param.16) | copy-start | bytes 52
  63.4 102.4 %all-gather.10.cloned.1.call-start = ((), (), s32[]{:S(2)}) async-start(), calls=%async_computation.4 | async-start | bytes 5308416 | tf_op jit(solution)/shard_map/all_gather | solution.py:107
  64.0 42.3 %copy-start.1 = (bf16[256,1536]{1,0:T(8,128)(2,1)S(1)}, bf16[256,1536]{1,0:T(8,128)(2,1)}, u32[]{:S(2)}) copy-start(bf16[256,1536]{1,0:T(8,128)(2,1)} %param.14) | copy-start | bytes 2359300
  64.0 42.3 %copy-start.4 = (f32[1536]{0:T(1024)S(1)}, f32[1536]{0:T(1024)}, u32[]{:S(2)}) copy-start(f32[1536]{0:T(1024)} %param.19) | copy-start | bytes 18436
  145.1 24.8 %copy-start.3 = (f32[1536]{0:T(1024)S(1)}, f32[1536]{0:T(1024)}, u32[]{:S(2)}) copy-start(f32[1536]{0:T(1024)} %param.24) | copy-start | bytes 18436
  169.9 65.5 %slice-start = ((s8[9437184]{0:T(1024)(128)(4,1)}), s8[4194304]{0:T(1024)(128)(4,1)S(1)}, s32[]{:S(2)}) async-start(s8[9437184]{0:T(1024)(128)(4,1)} %bitcast.80), calls=%async_computation.6 | async-start | bytes 8388608
  169.9 65.5 %slice-start.1 = ((s8[9437184]{0:T(1024)(128)(4,1)}), s8[4194304]{0:T(1024)(128)(4,1)S(1)}, s32[]{:S(2)}) async-start(s8[9437184]{0:T(1024)(128)(4,1)} %bitcast.80), calls=%async_computation.7 | async-start | bytes 8388608
  171.4 63.9 %slice-start.2 = ((s8[9437184]{0:T(1024)(128)(4,1)}), s8[1048576]{0:T(1024)(128)(4,1)S(1)}, s32[]{:S(2)}) async-start(s8[9437184]{0:T(1024)(128)(4,1)} %bitcast.80), calls=%async_computation.8 | async-start | bytes 2097152
  255.6 4.7 %copy-start.8 = (s32[1,16]{1,0:T(1,128)S(1)}, s32[1,16]{1,0:T(1,128)}, u32[]{:S(2)}) copy-start(s32[1,16]{1,0:T(1,128)} %param.17) | copy-start | bytes 196
  255.6 73.7 %all-to-all-start.1 = ((bf16[16,2,48,1536]{3,2,1,0:T(8,128)(2,1)}), bf16[16,2,48,1536]{3,2,1,0:T(8,128)(2,1)}, u32[]{:S(2)}, u32[]{:S(2)}) async-start(bf16[16,2,48,1536]{3,2,1,0:T(8,128)(2,1)} %copy.28), calls=%async_computation.1 | async-start | bytes 9437184 | tf_op jit(solution)/shard_map/all_to_all | solution.py:189
Sparse Core Ops, SparseCore 0:
  9.7 46.5 all-gather.5
  59.0 45.7 all-gather.11
  107.1 23.4 all-gather.7
  132.1 33.6 all-gather.9

commit v2 on v1

v2 whole, which is shorter than its diff:
```python
import jax
import jax.numpy as jnp
from jax import lax
from jax.experimental import pallas as pl
from jax.experimental.pallas import tpu as pltpu
from jax.sharding import PartitionSpec as P

HEAD_SIZE = 128
PAGE = 128
CAP = 48
SPAN = 1024

eps = 1e-06
neg_fill = -1e30


def rms_norm(values, gains):
    widened = values.astype(jnp.float32)
    inv_rms = lax.rsqrt(jnp.mean(widened * widened, axis=-1, keepdims=True) + eps)
    return (widened * inv_rms * gains).astype(jnp.bfloat16)


MESH = pl.DeviceIdType.MESH


class Ring:
    def __init__(self, buf, own, send, recv):
        me = lax.axis_index("mp")
        n = lax.axis_size("mp")
        chips = n // 2
        x, core = me // 2, lax.rem(me, 2)
        self.right = lax.rem(x + 1, chips) * 2 + core
        self.left = lax.rem(x + chips - 1, chips) * 2 + core
        self.far = lax.rem(x + 2, chips) * 2 + core
        self.me = me
        self.partner = x * 2 + 1 - core
        self.buf, self.own, self.send, self.recv = buf, own, send, recv
        self.half = buf.shape[1] // 2

    def other(self, slot):
        return slot + 1 - 2 * lax.rem(slot, 2)

    def copy(self, i, slot, part, target, own=False):
        rows = pl.ds(part * self.half, self.half)
        return pltpu.make_async_remote_copy(
            src_ref=self.own.at[rows] if own else self.buf.at[slot, rows],
            dst_ref=self.buf.at[slot, rows],
            send_sem=self.send.at[i],
            recv_sem=self.recv.at[i],
            device_id={"mp": target},
            device_id_type=MESH,
        )

    def begin(self):
        me = self.me
        self.copy(0, me, 0, self.right, True).start()
        self.copy(1, me, 1, self.left, True).start()
        self.copy(2, me, 1, self.right, True).start()
        self.copy(3, me, 0, self.left, True).start()
        self.copy(4, me, 0, self.partner, True).start()
        self.copy(5, me, 1, self.partner, True).start()

    def got(self, i, slot, part):
        self.copy(i, slot, part, self.partner).wait_recv()

    def got_partner(self):
        self.got(4, self.partner, 0)
        self.got(5, self.partner, 1)

    def forward_near(self):
        self.got(0, self.left, 0)
        self.copy(6, self.left, 0, self.right).start()
        self.copy(7, self.left, 0, self.partner).start()
        self.got(1, self.right, 1)
        self.copy(8, self.right, 1, self.left).start()
        self.copy(9, self.right, 1, self.partner).start()

    def forward_rest(self):
        self.got(2, self.left, 1)
        self.copy(10, self.left, 1, self.partner).start()
        self.got(3, self.right, 0)
        self.copy(11, self.right, 0, self.partner).start()

    def got_near(self):
        self.got(7, self.other(self.left), 0)
        self.got(10, self.other(self.left), 1)
        self.got(9, self.other(self.right), 1)
        self.got(11, self.other(self.right), 0)

    def forward_far(self):
        self.got(6, self.far, 0)
        self.copy(12, self.far, 0, self.partner).start()
        self.got(8, self.far, 1)
        self.copy(13, self.far, 1, self.partner).start()

    def got_far(self):
        self.got(12, self.other(self.far), 0)
        self.got(13, self.other(self.far), 1)

    def drain(self):
        for i in range(14):
            self.copy(i, self.me, 0, self.partner, True).wait_send()


HOPS = 14


def front_kernel(
    tokens_ref,
    gain_ref,
    weight_ref,
    packed_ref,
    adapter_ref,
    low_ref,
    out_weight_ref,
    residual_ref,
    kv_ref,
    weights,
    adapters,
    out_weights,
    qkv,
    query,
    attended,
    bias,
    normed,
    middle,
    weight_send,
    weight_recv,
    kv_send,
    kv_recv,
    out_send,
    out_recv,
    adapter_send,
    adapter_recv,
    local_sem,
):
    dp, mp = lax.axis_index("dp"), lax.axis_index("mp")
    n_dp = lax.axis_size("dp")
    n_mp = lax.axis_size("mp")
    rows, columns = tokens_ref.shape
    wide = weight_ref.shape[1]
    q_blocks = qkv.shape[0] - 2
    rank = packed_ref.shape[0] // 2

    ring = Ring(weights, weight_ref, weight_send, weight_recv)
    kv_ring = Ring(kv_ref, kv_ref.at[mp], kv_send, kv_recv)
    out_ring = Ring(out_weights, out_weight_ref, out_send, out_recv)

    barrier = pltpu.get_barrier_semaphore()
    for peer in (ring.left, ring.right, ring.partner):
        pl.semaphore_signal(barrier, inc=1, device_id={"mp": peer}, device_id_type=MESH)

    @pl.loop(1, n_dp)
    def _(k):
        peer = lax.rem(dp + k, n_dp)
        pl.semaphore_signal(barrier, inc=1, device_id={"dp": peer}, device_id_type=MESH)

    pl.semaphore_wait(barrier, 3 + n_dp - 1)

    def adapter_copy(k, slot, peer):
        return pltpu.make_async_remote_copy(
            src_ref=packed_ref,
            dst_ref=adapters.at[slot],
            send_sem=adapter_send.at[k],
            recv_sem=adapter_recv.at[slot],
            device_id={"dp": peer},
            device_id_type=MESH,
        )

    ring.begin()

    @pl.loop(1, n_dp)
    def _(k):
        adapter_copy(k, dp, lax.rem(dp + k, n_dp)).start()

    own_out = pltpu.make_async_copy(out_weight_ref, out_weights.at[mp], local_sem)
    own_out.start()
    adapters[dp] = packed_ref[...]

    widened = tokens_ref[...].astype(jnp.float32)
    inv_rms = lax.rsqrt(jnp.mean(widened * widened, axis=1, keepdims=True) + eps)
    normed[...] = (widened * inv_rms * gain_ref[...]).astype(jnp.bfloat16)

    window = bias.shape[1]
    first = jnp.maximum(mp + 1 - window // rows, 0)
    key = lax.broadcasted_iota(jnp.int32, (rows, window), 1) + first * rows
    place = lax.broadcasted_iota(jnp.int32, (rows, window), 0) + mp * rows
    bias[...] = jnp.where((key >= low_ref[...]) & (key <= place), 0.0, neg_fill)

    def project(slot):
        qkv[slot] = jnp.dot(normed[...], weights[slot], preferred_element_type=jnp.float32)

    qkv[mp] = jnp.dot(normed[...], weight_ref[...], preferred_element_type=jnp.float32)
    ring.got_partner()
    project(ring.partner)
    ring.forward_near()
    ring.forward_rest()
    project(ring.left)
    project(ring.right)

    @pl.loop(1, n_dp)
    def _(k):
        source = lax.rem(dp + k, n_dp)
        adapter_copy(k, source, source).wait_recv()

    down = adapters[:, :rank, :].reshape(n_dp * rank, columns)
    mid = lax.dot_general(
        normed[...], down, (((1,), (1,)), ((), ())), preferred_element_type=jnp.float32
    )
    owner = lax.broadcasted_iota(jnp.int32, (rows, n_dp * rank), 1) // rank
    middle[...] = jnp.where(owner == adapter_ref[...], mid, 0.0).astype(jnp.bfloat16)

    ring.got_near()
    project(ring.other(ring.left))
    project(ring.other(ring.right))
    ring.forward_far()
    project(ring.far)
    ring.got_far()
    project(ring.other(ring.far))

    kv_ref[mp, :, :wide] = qkv[q_blocks].astype(jnp.bfloat16)
    kv_ref[mp, :, wide:] = qkv[q_blocks + 1].astype(jnp.bfloat16)

    def finish_query(j):
        up = adapters[:, rank:, j * wide : (j + 1) * wide].reshape(n_dp * rank, wide)
        extra = jnp.dot(middle[...], up, preferred_element_type=jnp.float32)
        query[j] = (qkv[j] + extra).astype(jnp.bfloat16)

    finish_query(0)
    kv_ring.begin()
    for j in range(1, q_blocks):
        finish_query(j)
    kv_ring.forward_near()
    out_ring.begin()
    kv_ring.got_partner()
    kv_ring.forward_rest()
    kv_ring.got_near()
    kv_ring.forward_far()
    kv_ring.got_far()

    n_kv = 2
    share = q_blocks // n_kv
    for kv_head in range(n_kv):
        k_cols = slice(kv_head * HEAD_SIZE, (kv_head + 1) * HEAD_SIZE)
        v_cols = slice(wide + kv_head * HEAD_SIZE, wide + (kv_head + 1) * HEAD_SIZE)

        @pl.loop(0, share)
        def _(step):
            block = step + kv_head * share
            for lane in range(wide // HEAD_SIZE):
                cols = slice(lane * HEAD_SIZE, (lane + 1) * HEAD_SIZE)
                keys = kv_ref[pl.ds(first, window // rows), :, k_cols].reshape(window, HEAD_SIZE)
                values = kv_ref[pl.ds(first, window // rows), :, v_cols].reshape(window, HEAD_SIZE)
                scores = lax.dot_general(
                    query[block, :, cols],
                    keys,
                    (((1,), (1,)), ((), ())),
                    preferred_element_type=jnp.float32,
                )
                scores = scores + bias[...]
                row_max = jnp.max(scores, axis=1, keepdims=True)
                expd = jnp.exp((scores - row_max) * HEAD_SIZE ** (-0.5))
                total = jnp.sum(expd, axis=1, keepdims=True)
                mixed = jnp.dot(
                    expd.astype(jnp.bfloat16), values, preferred_element_type=jnp.float32
                )
                attended[block, :, cols] = (mixed / total).astype(jnp.bfloat16)

        if kv_head == 0:
            out_ring.forward_near()

    out_ring.forward_rest()
    out_ring.got_partner()
    out_ring.got_near()
    out_ring.forward_far()
    out_ring.got_far()
    own_out.wait()

    own_rows = out_weights.shape[1]
    for lo in range(0, n_mp, 2):
        part = out_weights[lo : lo + 2].reshape(2 * own_rows, columns)
        total = tokens_ref[:, lo * own_rows : (lo + 2) * own_rows].astype(jnp.float32)
        for j in range(q_blocks):
            total += lax.dot_general(
                attended[j],
                part[:, j * wide : (j + 1) * wide],
                (((1,), (1,)), ((), ())),
                preferred_element_type=jnp.float32,
            )
        residual_ref[:, lo * own_rows : (lo + 2) * own_rows] = total.astype(jnp.bfloat16)

    ring.drain()
    kv_ring.drain()
    out_ring.drain()

    @pl.loop(1, n_dp)
    def _(k):
        adapter_copy(k, dp, lax.rem(dp + k, n_dp)).wait_send()


def front(tokens, gain, weight, packed, adapter, low, out_weight):
    n_dp, n_mp = lax.axis_size("dp"), lax.axis_size("mp")
    rows, columns = tokens.shape
    depth, wide = weight.shape
    q_blocks = columns // wide
    window = min(n_mp * rows, rows + SPAN)
    dma = pltpu.SemaphoreType.DMA
    vmem = pl.BlockSpec(memory_space=pltpu.VMEM)
    return pl.pallas_call(
        front_kernel,
        in_specs=[vmem] * 7,
        out_specs=[vmem] * 2,
        out_shape=[
            jax.ShapeDtypeStruct((rows, columns), jnp.bfloat16),
            jax.ShapeDtypeStruct((n_mp, rows, 2 * wide), jnp.bfloat16),
        ],
        scratch_shapes=[
            pltpu.VMEM((n_mp, depth, wide), jnp.bfloat16),
            pltpu.VMEM((n_dp,) + packed.shape, jnp.bfloat16),
            pltpu.VMEM((n_mp,) + out_weight.shape, jnp.bfloat16),
            pltpu.VMEM((n_mp, rows, wide), jnp.float32),
            pltpu.VMEM((q_blocks, rows, wide), jnp.bfloat16),
            pltpu.VMEM((q_blocks, rows, wide), jnp.bfloat16),
            pltpu.VMEM((rows, window), jnp.float32),
            pltpu.VMEM((rows, columns), jnp.bfloat16),
            pltpu.VMEM((rows, n_dp * packed.shape[0] // 2), jnp.bfloat16),
            dma((HOPS,)),
            dma((HOPS,)),
            dma((HOPS,)),
            dma((HOPS,)),
            dma((HOPS,)),
            dma((HOPS,)),
            dma((n_dp,)),
            dma((n_dp,)),
            dma(()),
        ],
        compiler_params=pltpu.CompilerParams(
            collective_id=0, has_side_effects=True, vmem_limit_bytes=60 << 20
        ),
        name="front",
    )(tokens, gain, weight, packed, adapter, low, out_weight)


def shards(
    tokens,
    lengths,
    request_adapter,
    group_page_slots,
    routes,
    attention_gain,
    query_key_value_weight,
    adapter_down_weight,
    adapter_up_weight,
    output_weight,
    expert_norm_gain,
    router,
    expert_gate_up_weight,
    expert_down_weight,
):
    tokens_per_shard, model_columns = tokens.shape
    mp_index = lax.axis_index("mp")
    group_start = mp_index * tokens_per_shard
    n_exp = router.shape[1]

    packed = jnp.concatenate([adapter_down_weight[0].T, adapter_up_weight[0]], axis=0)

    seq_ends = jnp.sum(
        jnp.where(
            jnp.arange(lengths.shape[1])[:, None] <= jnp.arange(lengths.shape[1])[None, :],
            lengths[0][:, None],
            0,
        ),
        axis=0,
    )
    positions = group_start + jnp.arange(tokens_per_shard, dtype=jnp.int32)
    passed = positions[:, None] >= seq_ends[None, :]
    query_seg = jnp.sum(passed.astype(jnp.int32), axis=1)
    low = jnp.max(jnp.where(passed, seq_ends[None, :], 0), axis=1, keepdims=True)
    seq_match = query_seg[:, None] == jnp.arange(lengths.shape[1], dtype=jnp.int32)[None, :]
    token_adapter = jnp.sum(jnp.where(seq_match, request_adapter[0][None, :], 0), axis=1)

    residual, group_kv = front(
        tokens,
        attention_gain[None, :],
        query_key_value_weight,
        packed,
        token_adapter[:, None],
        low,
        output_weight.T,
    )

    pages_dev = tokens_per_shard // PAGE
    pages_grp = group_page_slots.shape[1]
    my_slots = mp_index * pages_dev + jnp.arange(pages_dev, dtype=jnp.int32)
    slot_match = (group_page_slots[0][None, :] == my_slots[:, None]).astype(jnp.int32)
    source_page = jnp.sum(slot_match * jnp.arange(pages_grp, dtype=jnp.int32)[None, :], axis=1)
    pages = group_kv.reshape(pages_grp, PAGE, group_kv.shape[2])
    pool = jnp.concatenate(
        [lax.dynamic_slice_in_dim(pages, source_page[i], 1, axis=0) for i in range(pages_dev)], axis=0
    )

    ffn_in = rms_norm(residual, expert_norm_gain)
    logits = jnp.dot(ffn_in, router, preferred_element_type=jnp.float32)
    hits = jnp.any(routes[:, :, None] == jnp.arange(n_exp, dtype=jnp.int32)[None, None, :], axis=1)
    peak = jnp.max(jnp.where(hits, logits, neg_fill), axis=1, keepdims=True)
    expl = jnp.where(hits, jnp.exp(jnp.where(hits, logits, peak) - peak), 0.0)
    route_weights = expl / jnp.sum(expl, axis=1, keepdims=True)
    before = (
        jnp.arange(tokens_per_shard)[None, :] < jnp.arange(tokens_per_shard)[:, None]
    ).astype(jnp.bfloat16)
    place = jnp.dot(before, hits.astype(jnp.bfloat16), preferred_element_type=jnp.float32)
    place = jnp.where(hits, place, -1.0).T
    chosen = place[:, None, :] == jnp.arange(CAP, dtype=jnp.int32).astype(jnp.float32)[None, :, None]
    send_map = chosen.astype(jnp.bfloat16).reshape(n_exp * CAP, tokens_per_shard)
    send_rows = jnp.dot(send_map, ffn_in, preferred_element_type=jnp.float32).astype(jnp.bfloat16)
    high = route_weights.astype(jnp.bfloat16)
    rest = (route_weights - high.astype(jnp.float32)).astype(jnp.bfloat16)
    zero = jnp.zeros((), jnp.bfloat16)
    back_high = jnp.where(chosen, high.T[:, None, :], zero).reshape(n_exp * CAP, tokens_per_shard)
    back_rest = jnp.where(chosen, rest.T[:, None, :], zero).reshape(n_exp * CAP, tokens_per_shard)

    n_dp = lax.axis_size("dp")
    exp_local = n_exp // n_dp
    outgoing = send_rows.reshape(n_dp, exp_local, CAP, model_columns)
    arrived = lax.all_to_all(outgoing, "dp", split_axis=0, concat_axis=0, tiled=True)
    gate_up = jnp.einsum(
        "secd,edf->secf", arrived, expert_gate_up_weight, preferred_element_type=jnp.float32
    )
    hidden_units = expert_down_weight.shape[1]
    active = (jnp.maximum(gate_up[..., :hidden_units], 0.0) * gate_up[..., hidden_units:]).astype(
        jnp.bfloat16
    )
    produced = jnp.einsum(
        "secf,efd->secd", active, expert_down_weight, preferred_element_type=jnp.float32
    ).astype(jnp.bfloat16)
    returned = lax.all_to_all(produced, "dp", split_axis=0, concat_axis=0, tiled=True)
    returned = returned.reshape(n_exp * CAP, model_columns)
    first_dim = (((0,), (0,)), ((), ()))
    mixture = lax.dot_general(back_high, returned, first_dim, preferred_element_type=jnp.float32)
    mixture = mixture + lax.dot_general(back_rest, returned, first_dim, preferred_element_type=jnp.float32)
    layer_out = (residual.astype(jnp.float32) + mixture).astype(jnp.bfloat16)
    return (layer_out, pool)


def solution(mesh):
    return jax.shard_map(
        shards,
        mesh=mesh,
        in_specs=(
            P(("dp", "mp"), None),
            P("dp", None),
            P("dp", None),
            P("dp", None),
            P(("dp", "mp"), None),
            P(),
            P(None, "mp"),
            P("dp", None, None),
            P("dp", None, None),
            P(None, "mp"),
            P(),
            P(),
            P("dp", None, None),
            P("dp", None, None),
        ),
        out_specs=(P(("dp", "mp"), None), P(("dp", "mp"), None, None)),
        check_vma=False,
    )
```

time: 347 us -> 246 us (0.71)
  waiting for transfers between devices: 189 us -> 60.8 us
  Pallas kernels: 14.6 us -> 73 us
  between operations: 17.9 us -> 4.7 us
  matrix products: 38.1 us -> 25.6 us
  blocking collectives: 63.9 us -> 60 us
  local copies, waits for them, and re-layouts: 11 us -> 7.18 us
    all_gather x4 -> x0, waiting for transfers between devices: 126 us -> none  [the longest x1 45.4 us: shards(): full_qkv = lax.all_gather(query_key_value_weight, 'mp', axis=1, tiled=True)]
    pallas_call x1, Pallas kernels: 14.6 us -> 73 us  [front(): pl.pallas_call(front_kernel, in_specs=[vmem] * 7, out_specs=[vmem] * 2, o...]
    dot_general x3 -> x0, matrix products: 12.3 us -> none  [the longest x1 4.89 us: shards(): qkv = jnp.dot(normed, full_qkv, preferred_element_type=jnp.float32)]
    all_to_all x1, blocking collectives: 63.9 us -> 60 us  [shards(): lax.all_to_all(outgoing, 'dp', split_axis=0, concat_axis=0, tiled=True)]
  transfers between devices with their start and end apart: 5 -> 1, of which waited for: 5 -> 1; matrix products, arithmetic and copies ran while one was open for 5% -> 1% of each run, Pallas kernels for 4% -> 0%
where the time goes in v2:
time: 246 us; the launch traced here: 243 us
  Pallas kernels  73 us (30%)
  waiting for transfers between devices  60.8 us (25%)
  blocking collectives  60 us (24%)
  matrix products  25.6 us (10%)
  local copies, waits for them, and re-layouts  7.18 us (3%)
  other arithmetic  6.69 us (3%)
  between operations  4.7 us (2%)
  starting transfers between devices  4.69 us (2%)
    pallas_call x1, Pallas kernels, front(): pl.pallas_call(front_kernel, in_specs=[vmem] * 7, out_specs=[vmem] * 2, o...  73 us
    all_to_all x1, waiting for transfers between devices, shards(): lax.all_to_all(produced, 'dp', split_axis=0, concat_axis=0, tiled=True)  60.8 us
    all_to_all x1, blocking collectives, shards(): lax.all_to_all(outgoing, 'dp', split_axis=0, concat_axis=0, tiled=True)  60 us
    dot_general x1, matrix products, shards(): jnp.einsum('secd,edf->secf', arrived, expert_gate_up_weight, preferred_el...  7.45 us
    dot_general x1, matrix products, shards(): jnp.einsum('secf,efd->secd', active, expert_down_weight, preferred_elemen...  6.37 us
  transfers between devices with their start and end apart: 1, of which 1 were waited for; matrix products, arithmetic and copies ran while one was open for 1% of the time, Pallas kernels for 0%

profile of v2, /device:TPU:6, one launch (start us, length us, event | category | flops | bytes accessed | tf_op | source)
XLA Modules:
  0.0 242.6 jit_solution(12669042042395702718)
XLA Ops:
  0.7 0.8 select_reduce_fusion.3
  1.4 1.3 broadcast_in_dim.102.gain_ref
  2.7 0.7 fusion.21
  3.8 0.7 select_reduce_fusion.2
  4.5 0.8 copy.28.adapter_ref
  5.3 0.8 copy.29.low_ref
  6.1 1.5 pad_maximum_fusion.1.packed_ref
  7.6 73.0 %front.1 = (bf16[256,1536]{1,0:T(8,128)(2,1)}, bf16[8,256,512]{2,1,0:T(8,128)(2,1)}) custom-call(bf16[256,1536]{1,0:T(8,128)(2,1)} %tokens_ref.1, f32[1,1536]{1,0:T(1,128)} %broadcast_in_dim.102.gain_ref, bf16[1536,256]{1,0:T(8,128)(2,1)} %weight_ref.1, bf16[32,1536]{1,0:T(8,128)(2,1)} %pad_maximum_fusion.1.packed_ref, s32[256,1]{1,0:T(8,128)} %copy.28.adapter_ref, ...), custom_call_target="tpu_custom_call" | custom-call | tf_op jit(solution)/shard_map/front/pallas_call | solution.py:309
  80.6 1.4 fusion.15
  82.0 0.3 bitcast_compare_fusion
  82.3 2.8 %convolution_convert_fusion = bf16[1536,1536]{1,0:T(8,128)(2,1)S(1)} fusion(pred[1536,256]{1,0:T(32,128)(4,1)S(1)} %bitcast_compare_fusion, bf16[256,1536]{1,0:T(8,128)(2,1)} %get-tuple-element.4, f32[1536]{0:T(1024)} %param.24, f32[256]{0:T(256)S(1)} %add_rsqrt_fusion), kind=kOutput, calls=%fused_computation.2 | convolution fusion | flops 1211891712 | bytes 5905408 | tf_op jit(solution)/shard_map/dot_general | solution.py:415
  85.1 60.0 %all_to_all.10 = bf16[16,2,48,1536]{3,2,1,0:T(8,128)(2,1)S(1)} all-to-all(bf16[16,2,48,1536]{3,2,1,0:T(8,128)(2,1)S(1)} %bitcast.71), channel_id=1, replica_groups=mesh['dp'=16,'mp'=8] {'dp'}, dimensions={0} | all-to-all | bytes 9437184 | tf_op jit(solution)/shard_map/all_to_all | solution.py:425
  145.1 7.5 %fusion.2 = f32[16,2,48,1536]{3,2,0,1:T(8,128)S(1)} fusion(bf16[2,1536,1536]{2,1,0:T(8,128)(2,1)S(1)} %bitcast.73, bf16[16,2,48,1536]{3,2,1,0:T(8,128)(2,1)S(1)} %all_to_all.10), kind=kOutput, calls=%fused_computation.3 | convolution fusion | flops 7247757312 | bytes 23592960 | tf_op jit(solution)/shard_map/secd,edf->secf/dot_general | solution.py:426
  152.6 6.4 %convert_bitcast_fusion = bf16[16,2,48,1536]{3,2,0,1:T(8,128)(2,1)S(1)} fusion(bf16[2,768,1536]{2,1,0:T(8,128)(2,1)} %param.27, f32[16,2,48,1536]{3,2,0,1:T(8,128)S(1)} %fusion.2), kind=kOutput, calls=%fused_computation.10 | convolution fusion | flops 3629776896 | bytes 18874368 | tf_op jit(solution)/shard_map/secf,efd->secd/dot_general | solution.py:433
  159.0 2.6 %copy.31 = bf16[16,2,48,1536]{3,2,1,0:T(8,128)(2,1)} copy(bf16[16,2,48,1536]{3,2,0,1:T(8,128)(2,1)S(1)} %convert_bitcast_fusion) | data formatting | bytes 9437184 | tf_op jit(solution)/shard_map/convert_element_type | solution.py:435
  161.6 4.7 %all-to-all-start.1 = ((bf16[16,2,48,1536]{3,2,1,0:T(8,128)(2,1)}), bf16[16,2,48,1536]{3,2,1,0:T(8,128)(2,1)}, u32[]{:S(2)}, u32[]{:S(2)}) async-start(bf16[16,2,48,1536]{3,2,1,0:T(8,128)(2,1)} %copy.31), calls=%async_computation.1 | async-start | bytes 9437184 | tf_op jit(solution)/shard_map/all_to_all | solution.py:436
  166.5 0.6 fusion.31
  171.0 0.4 select_reduce_fusion.1
  171.4 1.0 constant_dynamic-slice_fusion
  172.4 0.7 pad_maximum_fusion
  173.2 0.3 compare_select_fusion
  173.5 60.8 %all-to-all-done.1 = bf16[16,2,48,1536]{3,2,1,0:T(8,128)(2,1)} async-done(((bf16[16,2,48,1536]{3,2,1,0:T(8,128)(2,1)}), bf16[16,2,48,1536]{3,2,1,0:T(8,128)(2,1)}, u32[]{:S(2)}, u32[]{:S(2)}) %all-to-all-start.1) | async-done | bytes 4718624 | tf_op jit(solution)/shard_map/all_to_all | solution.py:436
  234.3 3.7 %fusion.32 = f32[256,1536]{1,0:T(8,128)S(1)} fusion(bf16[1536,256]{1,0:T(8,128)(2,1)S(1)} %bitcast.75, bf16[1536,1536]{1,0:T(8,128)(2,1)} %bitcast.19), kind=kOutput, calls=%fused_computation.57 | convolution fusion | flops 1207959552 | bytes 7077888 | tf_op jit(solution)/shard_map/dot_general | solution.py:439
  238.0 4.6 %fusion.12 = bf16[256,1536]{1,0:T(8,128)(2,1)} fusion(f32[256,1536]{1,0:T(8,128)S(1)} %fusion.32, bf16[1536,256]{1,0:T(8,128)(2,1)S(1)} %bitcast.74, bf16[1536,1536]{1,0:T(8,128)(2,1)} %bitcast.19, bf16[256,1536]{1,0:T(8,128)(2,1)S(1)} %copy-done.1), kind=kOutput, calls=%fused_computation.13 | convolution fusion | flops 1209532416 | bytes 8650752 | tf_op jit(solution)/shard_map/dot_general | solution.py:440
  (26 shorter events, 0.6 us)
Async XLA Ops:
  0.6 170.3 %copy-start = (bf16[1536,32]{0,1:T(8,128)(2,1)S(1)}, bf16[1536,32]{0,1:T(8,128)(2,1)}, u32[]{:S(2)}) copy-start(bf16[1536,32]{0,1:T(8,128)(2,1)} %param.25) | copy-start | bytes 294916
  82.3 62.8 %slice-start = ((s8[9437184]{0:T(1024)(128)(4,1)}), s8[4194304]{0:T(1024)(128)(4,1)S(1)}, s32[]{:S(2)}) async-start(s8[9437184]{0:T(1024)(128)(4,1)} %bitcast.72), calls=%async_computation.2 | async-start | bytes 8388608
  82.3 62.8 %slice-start.1 = ((s8[9437184]{0:T(1024)(128)(4,1)}), s8[4194304]{0:T(1024)(128)(4,1)S(1)}, s32[]{:S(2)}) async-start(s8[9437184]{0:T(1024)(128)(4,1)} %bitcast.72), calls=%async_computation.3 | async-start | bytes 8388608
  85.1 60.0 %slice-start.2 = ((s8[9437184]{0:T(1024)(128)(4,1)}), s8[1048576]{0:T(1024)(128)(4,1)S(1)}, s32[]{:S(2)}) async-start(s8[9437184]{0:T(1024)(128)(4,1)} %bitcast.72), calls=%async_computation.4 | async-start | bytes 2097152
  161.5 4.7 %copy-start.3 = (s32[1,16]{1,0:T(1,128)S(1)}, s32[1,16]{1,0:T(1,128)}, u32[]{:S(2)}) copy-start(s32[1,16]{1,0:T(1,128)} %param.17) | copy-start | bytes 196
  161.5 9.4 %copy-start.1 = (bf16[256,1536]{1,0:T(8,128)(2,1)S(1)}, bf16[256,1536]{1,0:T(8,128)(2,1)}, u32[]{:S(2)}) copy-start(bf16[256,1536]{1,0:T(8,128)(2,1)} %get-tuple-element.4) | copy-start | bytes 2359300
  161.5 9.4 %copy-start.2 = (f32[1536]{0:T(1024)S(1)}, f32[1536]{0:T(1024)}, u32[]{:S(2)}) copy-start(f32[1536]{0:T(1024)} %param.24) | copy-start | bytes 18436
  161.6 72.7 %all-to-all-start.1 = ((bf16[16,2,48,1536]{3,2,1,0:T(8,128)(2,1)}), bf16[16,2,48,1536]{3,2,1,0:T(8,128)(2,1)}, u32[]{:S(2)}, u32[]{:S(2)}) async-start(bf16[16,2,48,1536]{3,2,1,0:T(8,128)(2,1)} %copy.31), calls=%async_computation.1 | async-start | bytes 9437184 | tf_op jit(solution)/shard_map/all_to_all | solution.py:436

commit v3 on v2

--- a/solution.py
+++ b/solution.py
@@ -341,6 +341,199 @@
     )(tokens, gain, weight, packed, adapter, low, out_weight)
 
 
+ORDER = (0, 10, 11, 9, 14, 6, 2, 8, 5, 7, 13, 15, 1, 3, 4, 12)
+PIECE = 16
+
+
+def expert_kernel(
+    ffn_ref,
+    map_ref,
+    back_ref,
+    rest_ref,
+    residual_ref,
+    up_hbm,
+    down_hbm,
+    out_ref,
+    sent,
+    arrived,
+    produced,
+    returned,
+    up,
+    down,
+    active,
+    back,
+    total,
+    go_send,
+    go_recv,
+    back_send,
+    back_recv,
+    local_sem,
+):
+    dp = lax.axis_index("dp")
+    n_local, n_dp, cap, columns = sent.shape
+    side = 4
+    z, y = dp // side, lax.rem(dp, side)
+    slots = n_dp * cap
+    hidden = down.shape[1]
+    rows = ffn_ref.shape[0]
+    tile = 512
+
+    def toward(k):
+        return lax.rem(z + k // side, side) * side + lax.rem(y + k % side, side)
+
+    def source(k):
+        return (
+            lax.rem(z + side - k // side, side) * side + lax.rem(y + side - k % side, side)
+        )
+
+    owners = [toward(k) for k in ORDER]
+
+    barrier = pltpu.get_barrier_semaphore()
+
+    @pl.loop(1, n_dp)
+    def _(k):
+        peer = lax.rem(dp + k, n_dp)
+        pl.semaphore_signal(barrier, inc=1, device_id={"dp": peer}, device_id_type=MESH)
+
+    up_copy = pltpu.make_async_copy(up_hbm, up, local_sem.at[0])
+    down_copy = pltpu.make_async_copy(down_hbm, down, local_sem.at[1])
+    up_copy.start()
+    down_copy.start()
+
+    def transfer(src, dst, send, recv, e, pos, piece, peer):
+        part = pl.ds(piece * PIECE, PIECE)
+        return pltpu.make_async_remote_copy(
+            src_ref=src.at[e, pos, part],
+            dst_ref=dst.at[e, pos, part],
+            send_sem=send.at[e],
+            recv_sem=recv.at[e],
+            device_id={"dp": peer},
+            device_id_type=MESH,
+        )
+
+    def whole(src, dst, send, recv, e):
+        return pltpu.make_async_remote_copy(
+            src_ref=src.at[e, 1:],
+            dst_ref=dst.at[e, 1:],
+            send_sem=send.at[e],
+            recv_sem=recv.at[e],
+            device_id={"dp": owners[1]},
+            device_id_type=MESH,
+        )
+
+    def pack(e):
+        pick = jnp.concatenate([map_ref[owner, e] for owner in owners], axis=0)
+
+        @pl.loop(0, columns // tile)
+        def _(j):
+            cols = pl.ds(pl.multiple_of(j * tile, tile), tile)
+            got = jnp.dot(pick, ffn_ref[:, cols], preferred_element_type=jnp.float32)
+            sent[e, :, :, cols] = got.astype(jnp.bfloat16).reshape(n_dp, cap, tile)
+
+    def dispatch(e):
+        for piece in range(cap // PIECE):
+            for pos in range(1, n_dp):
+                transfer(sent, arrived, go_send, go_recv, e, pos, piece, owners[pos]).start()
+
+    def give_back(e):
+        for piece in range(cap // PIECE):
+            for pos in range(1, n_dp):
+                peer = source(ORDER[pos])
+                transfer(produced, returned, back_send, back_recv, e, pos, piece, peer).start()
+
+    def compute(e):
+        arrived[e, 0] = sent[e, 0]
+
+        @pl.loop(0, hidden // 256)
+        def _(j):
+            gate_cols = pl.ds(pl.multiple_of(j * 256, 256), 256)
+            up_cols = pl.ds(pl.multiple_of(hidden + j * 256, 256), 256)
+            given = arrived[e].reshape(slots, columns)
+            gate = jnp.dot(given, up[e, :, gate_cols], preferred_element_type=jnp.float32)
+            lift = jnp.dot(given, up[e, :, up_cols], preferred_element_type=jnp.float32)
+            active[:, gate_cols] = (jnp.maximum(gate, 0.0) * lift).astype(jnp.bfloat16)
+
+        @pl.loop(0, columns // 256)
+        def _(j):
+            cols = pl.ds(pl.multiple_of(j * 256, 256), 256)
+            made = jnp.dot(active[...], down[e, :, cols], preferred_element_type=jnp.float32)
+            produced[e, :, :, cols] = made.astype(jnp.bfloat16).reshape(n_dp, cap, 256)
+
+        returned[e, 0] = produced[e, 0]
+
+    def combine(e):
+        @pl.loop(0, columns // tile)
+        def _(j):
+            cols = pl.ds(pl.multiple_of(j * tile, tile), tile)
+            given = returned[e, :, :, cols].reshape(slots, tile)
+            mixed = jnp.dot(back[e, 0], given, preferred_element_type=jnp.float32)
+            mixed += jnp.dot(back[e, 1], given, preferred_element_type=jnp.float32)
+            if e == 0:
+                total[:, cols] = residual_ref[:, cols].astype(jnp.float32) + mixed
+            else:
+                out_ref[:, cols] = (total[:, cols] + mixed).astype(jnp.bfloat16)
+
+    pack(0)
+    pl.semaphore_wait(barrier, n_dp - 1)
+    dispatch(0)
+    pack(1)
+    for e in range(n_local):
+        for i, ref in enumerate((back_ref, rest_ref)):
+            joined = jnp.concatenate([ref[owner, e] for owner in owners], axis=0)
+            back[e, i] = joined.T
+        if e == 0:
+            dispatch(1)
+    up_copy.wait()
+    down_copy.wait()
+    for e in range(n_local):
+        whole(sent, arrived, go_send, go_recv, e).wait_recv()
+        compute(e)
+        give_back(e)
+    for e in range(n_local):
+        whole(produced, returned, back_send, back_recv, e).wait_recv()
+        combine(e)
+    for e in range(n_local):
+        whole(sent, arrived, go_send, go_recv, e).wait_send()
+        whole(produced, returned, back_send, back_recv, e).wait_send()
+
+
+def experts(ffn_in, send_map, back_high, back_rest, residual, gate_up_weight, down_weight):
+    rows, columns = ffn_in.shape
+    n_dp = lax.axis_size("dp")
+    n_local, hidden = down_weight.shape[:2]
+    dma = pltpu.SemaphoreType.DMA
+    vmem = pl.BlockSpec(memory_space=pltpu.VMEM)
+    hbm = pl.BlockSpec(memory_space=pl.ANY)
+    block = (n_local, n_dp, CAP, columns)
+    maps = [m.reshape(n_dp, n_local, CAP, rows) for m in (send_map, back_high, back_rest)]
+    return pl.pallas_call(
+        expert_kernel,
+        in_specs=[vmem] * 5 + [hbm] * 2,
+        out_specs=vmem,
+        out_shape=jax.ShapeDtypeStruct((rows, columns), jnp.bfloat16),
+        scratch_shapes=[
+            pltpu.VMEM(block, jnp.bfloat16),
+            pltpu.VMEM(block, jnp.bfloat16),
+            pltpu.VMEM(block, jnp.bfloat16),
+            pltpu.VMEM(block, jnp.bfloat16),
+            pltpu.VMEM(gate_up_weight.shape, jnp.bfloat16),
+            pltpu.VMEM(down_weight.shape, jnp.bfloat16),
+            pltpu.VMEM((n_dp * CAP, hidden), jnp.bfloat16),
+            pltpu.VMEM((n_local, 2, rows, n_dp * CAP), jnp.bfloat16),
+            pltpu.VMEM((rows, columns), jnp.float32),
+            dma((n_local,)),
+            dma((n_local,)),
+            dma((n_local,)),
+            dma((n_local,)),
+            dma((2,)),
+        ],
+        compiler_params=pltpu.CompilerParams(
+            collective_id=1, has_side_effects=True, vmem_limit_bytes=60 << 20
+        ),
+        name="experts",
+    )(ffn_in, *maps, residual, gate_up_weight, down_weight)
+
+
 def shards(
     tokens,
     lengths,
@@ -412,33 +605,15 @@
     place = jnp.where(hits, place, -1.0).T
     chosen = place[:, None, :] == jnp.arange(CAP, dtype=jnp.int32).astype(jnp.float32)[None, :, None]
     send_map = chosen.astype(jnp.bfloat16).reshape(n_exp * CAP, tokens_per_shard)
-    send_rows = jnp.dot(send_map, ffn_in, preferred_element_type=jnp.float32).astype(jnp.bfloat16)
     high = route_weights.astype(jnp.bfloat16)
     rest = (route_weights - high.astype(jnp.float32)).astype(jnp.bfloat16)
     zero = jnp.zeros((), jnp.bfloat16)
     back_high = jnp.where(chosen, high.T[:, None, :], zero).reshape(n_exp * CAP, tokens_per_shard)
     back_rest = jnp.where(chosen, rest.T[:, None, :], zero).reshape(n_exp * CAP, tokens_per_shard)
 
-    n_dp = lax.axis_size("dp")
-    exp_local = n_exp // n_dp
-    outgoing = send_rows.reshape(n_dp, exp_local, CAP, model_columns)
-    arrived = lax.all_to_all(outgoing, "dp", split_axis=0, concat_axis=0, tiled=True)
-    gate_up = jnp.einsum(
-        "secd,edf->secf", arrived, expert_gate_up_weight, preferred_element_type=jnp.float32
+    layer_out = experts(
+        ffn_in, send_map, back_high, back_rest, residual, expert_gate_up_weight, expert_down_weight
     )
-    hidden_units = expert_down_weight.shape[1]
-    active = (jnp.maximum(gate_up[..., :hidden_units], 0.0) * gate_up[..., hidden_units:]).astype(
-        jnp.bfloat16
-    )
-    produced = jnp.einsum(
-        "secf,efd->secd", active, expert_down_weight, preferred_element_type=jnp.float32
-    ).astype(jnp.bfloat16)
-    returned = lax.all_to_all(produced, "dp", split_axis=0, concat_axis=0, tiled=True)
-    returned = returned.reshape(n_exp * CAP, model_columns)
-    first_dim = (((0,), (0,)), ((), ()))
-    mixture = lax.dot_general(back_high, returned, first_dim, preferred_element_type=jnp.float32)
-    mixture = mixture + lax.dot_general(back_rest, returned, first_dim, preferred_element_type=jnp.float32)
-    layer_out = (residual.astype(jnp.float32) + mixture).astype(jnp.bfloat16)
     return (layer_out, pool)
 
 

time: 246 us -> 207 us (0.84)
  Pallas kernels: 73 us -> 185 us
  waiting for transfers between devices: 60.8 us -> 0 us
  blocking collectives: 60 us -> 0 us
  matrix products: 25.6 us -> 0.52 us
  starting transfers between devices: 4.69 us -> 0 us
    pallas_call x0 -> x1, Pallas kernels: none -> 112 us  [experts(): pl.pallas_call(expert_kernel, in_specs=[vmem] * 5 + [hbm] * 2, out_specs=...]
    all_to_all x1 -> x0, waiting for transfers between devices: 60.8 us -> none  [shards(): lax.all_to_all(produced, 'dp', split_axis=0, concat_axis=0, tiled=True)]
    all_to_all x1 -> x0, blocking collectives: 60 us -> none  [shards(): lax.all_to_all(outgoing, 'dp', split_axis=0, concat_axis=0, tiled=True)]
    dot_general x5 -> x0, matrix products: 25 us -> none  [the longest x1 7.45 us: shards(): jnp.einsum('secd,edf->secf', arrived, expert_gate_up_weight, preferred_el...]
    all_to_all x1 -> x0, starting transfers between devices: 4.69 us -> none  [shards(): lax.all_to_all(produced, 'dp', split_axis=0, concat_axis=0, tiled=True)]
    convert_element_type x1 -> x0, local copies, waits for them, and re-layouts: 2.59 us -> none  [shards(): produced = jnp.einsum('secf,efd->secd', active, expert_down_weight, prefe...]
  transfers between devices with their start and end apart: 1 -> 0, of which waited for: 1 -> 0; matrix products, arithmetic and copies ran while one was open for 1% -> 0% of each run, Pallas kernels for 0% -> 0%
where the time goes in v3:
time: 207 us; the launch traced here: 205 us
  Pallas kernels  185 us (89%)
  other arithmetic  8.46 us (4%)
  local copies, waits for them, and re-layouts  6.71 us (3%)
  between operations  4.63 us (2%)
    pallas_call x1, Pallas kernels, experts(): pl.pallas_call(expert_kernel, in_specs=[vmem] * 5 + [hbm] * 2, out_specs=...  112 us
    pallas_call x1, Pallas kernels, front(): pl.pallas_call(front_kernel, in_specs=[vmem] * 7, out_specs=[vmem] * 2, o...  73 us

profile of v3, /device:TPU:6, one launch (start us, length us, event | category | flops | bytes accessed | tf_op | source)
XLA Modules:
  0.0 204.9 jit_solution(8242177351965414076)
XLA Ops:
  0.6 0.0 copy-start
  0.7 0.9 fusion.10
  1.5 0.7 select_reduce_fusion.3
  2.3 0.1 fusion.9
  2.4 0.6 fusion.12
  6.8 0.7 select_reduce_fusion.2
  7.6 1.3 broadcast_in_dim.106.gain_ref
  8.9 0.7 fusion.3
  9.6 0.2 convolution_select_fusion
  9.8 1.5 pad_maximum_fusion.1.packed_ref
  11.3 0.8 copy.20.adapter_ref
  12.1 0.8 copy.21.low_ref
  12.9 1.1 compare_convert_fusion.map_ref
  14.0 73.0 %front.1 = (bf16[256,1536]{1,0:T(8,128)(2,1)}, bf16[8,256,512]{2,1,0:T(8,128)(2,1)}) custom-call(bf16[256,1536]{1,0:T(8,128)(2,1)} %tokens_ref.1, f32[1,1536]{1,0:T(1,128)} %broadcast_in_dim.106.gain_ref, bf16[1536,256]{1,0:T(8,128)(2,1)} %weight_ref.1, bf16[32,1536]{1,0:T(8,128)(2,1)} %pad_maximum_fusion.1.packed_ref, s32[256,1]{1,0:T(8,128)} %copy.20.adapter_ref, ...), custom_call_target="tpu_custom_call" | custom-call | tf_op jit(solution)/shard_map/front/pallas_call | solution.py:309
  87.1 1.1 constant_dynamic-slice_fusion
  88.1 0.7 pad_maximum_fusion
  88.8 0.0 copy-done.1
  88.9 0.2 fusion
  89.1 0.2 fusion.2.ffn_ref
  89.4 0.0 copy-start.2
  89.4 0.4 select_reduce_fusion.1
  89.8 1.4 compare_select_fusion
  91.3 111.5 %experts.1 = bf16[256,1536]{1,0:T(8,128)(2,1)} custom-call(bf16[256,1536]{1,0:T(8,128)(2,1)} %copy-done.2, bf16[16,2,48,256]{3,2,1,0:T(8,128)(2,1)} %compare_convert_fusion.map_ref, bf16[16,2,48,256]{3,2,1,0:T(8,128)(2,1)} %get-tuple-element.13.back_ref, bf16[16,2,48,256]{3,2,1,0:T(8,128)(2,1)} %get-tuple-element.12.rest_ref, ...), custom_call_target="tpu_custom_call" | custom-call | tf_op jit(solution)/shard_map/experts/pallas_call | solution.py:509
  202.8 2.1 %copy.23 = bf16[256,1536]{1,0:T(8,128)(2,1)} copy(bf16[256,1536]{1,0:T(8,128)(2,1)} %experts.1) | data formatting | bytes 1572864
  (14 shorter events, 0.2 us)
Async XLA Ops:
  0.6 88.7 %copy-start = (bf16[1536,32]{0,1:T(8,128)(2,1)S(1)}, bf16[1536,32]{0,1:T(8,128)(2,1)}, u32[]{:S(2)}) copy-start(bf16[1536,32]{0,1:T(8,128)(2,1)} %param.25) | copy-start | bytes 294916
  14.0 75.1 %copy-start.3 = (f32[1536]{0:T(1024)S(1)}, f32[1536]{0:T(1024)}, u32[]{:S(2)}) copy-start(f32[1536]{0:T(1024)} %param.24) | copy-start | bytes 18436
  87.0 1.8 copy-start.1
  89.4 1.9 copy-start.2

commit v4 on v3

--- a/solution.py
+++ b/solution.py
@@ -12,12 +12,6 @@
 
 eps = 1e-06
 neg_fill = -1e30
-
-
-def rms_norm(values, gains):
-    widened = values.astype(jnp.float32)
-    inv_rms = lax.rsqrt(jnp.mean(widened * widened, axis=-1, keepdims=True) + eps)
-    return (widened * inv_rms * gains).astype(jnp.bfloat16)
 
 
 MESH = pl.DeviceIdType.MESH
@@ -109,9 +103,10 @@
     tokens_ref,
     gain_ref,
     weight_ref,
-    packed_ref,
-    adapter_ref,
-    low_ref,
+    down_ref,
+    up_ref,
+    lengths_ref,
+    request_ref,
     out_weight_ref,
     residual_ref,
     kv_ref,
@@ -124,6 +119,7 @@
     bias,
     normed,
     middle,
+    packed_ref,
     weight_send,
     weight_recv,
     kv_send,
@@ -140,7 +136,7 @@
     rows, columns = tokens_ref.shape
     wide = weight_ref.shape[1]
     q_blocks = qkv.shape[0] - 2
-    rank = packed_ref.shape[0] // 2
+    rank = up_ref.shape[1]
 
     ring = Ring(weights, weight_ref, weight_send, weight_recv)
     kv_ring = Ring(kv_ref, kv_ref.at[mp], kv_send, kv_recv)
@@ -169,23 +165,36 @@
 
     ring.begin()
 
+    packed_ref[rank:, :] = up_ref[0]
+    packed_ref[:rank, :] = down_ref[0].astype(jnp.float32).T.astype(jnp.bfloat16)
+
+    own_out = pltpu.make_async_copy(out_weight_ref, out_weights.at[mp], local_sem)
+    own_out.start()
+
+    widened = tokens_ref[...].astype(jnp.float32)
+    inv_rms = lax.rsqrt(jnp.mean(widened * widened, axis=1, keepdims=True) + eps)
+    normed[...] = (widened * inv_rms * gain_ref[...][None, :]).astype(jnp.bfloat16)
+
     @pl.loop(1, n_dp)
     def _(k):
         adapter_copy(k, dp, lax.rem(dp + k, n_dp)).start()
 
-    own_out = pltpu.make_async_copy(out_weight_ref, out_weights.at[mp], local_sem)
-    own_out.start()
     adapters[dp] = packed_ref[...]
 
-    widened = tokens_ref[...].astype(jnp.float32)
-    inv_rms = lax.rsqrt(jnp.mean(widened * widened, axis=1, keepdims=True) + eps)
-    normed[...] = (widened * inv_rms * gain_ref[...]).astype(jnp.bfloat16)
+    place = lax.broadcasted_iota(jnp.int32, (rows, 1), 0) + mp * rows
+    low = jnp.zeros((rows, 1), jnp.int32)
+    adapter = jnp.zeros((rows, 1), jnp.int32) + request_ref[:, 0:1]
+    ends = jnp.zeros((1, 1), jnp.int32)
+    for r in range(1, lengths_ref.shape[1]):
+        ends = ends + lengths_ref[:, r - 1 : r]
+        passed = place >= ends
+        low = jnp.where(passed, ends, low)
+        adapter = jnp.where(passed, request_ref[:, r : r + 1], adapter)
 
     window = bias.shape[1]
     first = jnp.maximum(mp + 1 - window // rows, 0)
     key = lax.broadcasted_iota(jnp.int32, (rows, window), 1) + first * rows
-    place = lax.broadcasted_iota(jnp.int32, (rows, window), 0) + mp * rows
-    bias[...] = jnp.where((key >= low_ref[...]) & (key <= place), 0.0, neg_fill)
+    bias[...] = jnp.where((key >= low) & (key <= place), 0.0, neg_fill)
 
     def project(slot):
         qkv[slot] = jnp.dot(normed[...], weights[slot], preferred_element_type=jnp.float32)
@@ -208,7 +217,7 @@
         normed[...], down, (((1,), (1,)), ((), ())), preferred_element_type=jnp.float32
     )
     owner = lax.broadcasted_iota(jnp.int32, (rows, n_dp * rank), 1) // rank
-    middle[...] = jnp.where(owner == adapter_ref[...], mid, 0.0).astype(jnp.bfloat16)
+    middle[...] = jnp.where(owner == adapter, mid, 0.0).astype(jnp.bfloat16)
 
     ring.got_near()
     project(ring.other(ring.left))
@@ -298,17 +307,18 @@
         adapter_copy(k, dp, lax.rem(dp + k, n_dp)).wait_send()
 
 
-def front(tokens, gain, weight, packed, adapter, low, out_weight):
+def front(tokens, gain, weight, down, up, lengths, request, out_weight):
     n_dp, n_mp = lax.axis_size("dp"), lax.axis_size("mp")
     rows, columns = tokens.shape
     depth, wide = weight.shape
     q_blocks = columns // wide
+    rank = up.shape[1]
     window = min(n_mp * rows, rows + SPAN)
     dma = pltpu.SemaphoreType.DMA
     vmem = pl.BlockSpec(memory_space=pltpu.VMEM)
     return pl.pallas_call(
         front_kernel,
-        in_specs=[vmem] * 7,
+        in_specs=[vmem] * 8,
         out_specs=[vmem] * 2,
         out_shape=[
             jax.ShapeDtypeStruct((rows, columns), jnp.bfloat16),
@@ -316,14 +326,15 @@
         ],
         scratch_shapes=[
             pltpu.VMEM((n_mp, depth, wide), jnp.bfloat16),
-            pltpu.VMEM((n_dp,) + packed.shape, jnp.bfloat16),
+            pltpu.VMEM((n_dp, 2 * rank, columns), jnp.bfloat16),
             pltpu.VMEM((n_mp,) + out_weight.shape, jnp.bfloat16),
             pltpu.VMEM((n_mp, rows, wide), jnp.float32),
             pltpu.VMEM((q_blocks, rows, wide), jnp.bfloat16),
             pltpu.VMEM((q_blocks, rows, wide), jnp.bfloat16),
             pltpu.VMEM((rows, window), jnp.float32),
             pltpu.VMEM((rows, columns), jnp.bfloat16),
-            pltpu.VMEM((rows, n_dp * packed.shape[0] // 2), jnp.bfloat16),
+            pltpu.VMEM((rows, n_dp * rank), jnp.bfloat16),
+            pltpu.VMEM((2 * rank, columns), jnp.bfloat16),
             dma((HOPS,)),
             dma((HOPS,)),
             dma((HOPS,)),
@@ -338,7 +349,7 @@
             collective_id=0, has_side_effects=True, vmem_limit_bytes=60 << 20
         ),
         name="front",
-    )(tokens, gain, weight, packed, adapter, low, out_weight)
+    )(tokens, gain, weight, down, up, lengths, request, out_weight)
 
 
 ORDER = (0, 10, 11, 9, 14, 6, 2, 8, 5, 7, 13, 15, 1, 3, 4, 12)
@@ -346,14 +357,16 @@
 
 
 def expert_kernel(
-    ffn_ref,
-    map_ref,
-    back_ref,
-    rest_ref,
     residual_ref,
+    gain_ref,
+    router_ref,
+    routes_ref,
+    page_slots_ref,
+    kv_hbm,
     up_hbm,
     down_hbm,
     out_ref,
+    pool_ref,
     sent,
     arrived,
     produced,
@@ -363,6 +376,12 @@
     active,
     back,
     total,
+    ffn_ref,
+    pages,
+    flat,
+    places,
+    high,
+    rest,
     go_send,
     go_recv,
     back_send,
@@ -376,6 +395,7 @@
     slots = n_dp * cap
     hidden = down.shape[1]
     rows = ffn_ref.shape[0]
+    n_exp = n_local * n_dp
     tile = 512
 
     def toward(k):
@@ -397,8 +417,38 @@
 
     up_copy = pltpu.make_async_copy(up_hbm, up, local_sem.at[0])
     down_copy = pltpu.make_async_copy(down_hbm, down, local_sem.at[1])
+    kv_copy = pltpu.make_async_copy(kv_hbm, pages, local_sem.at[2])
     up_copy.start()
     down_copy.start()
+    kv_copy.start()
+
+    def flip(values):
+        flat[:, : values.shape[1]] = values
+        return flat[...].T[: values.shape[1]]
+
+    def spread(table, e):
+        return [
+            jnp.broadcast_to(table[pl.ds(owner * n_local + e, 1), :], (cap, rows))
+            for owner in owners
+        ]
+
+    count = lax.broadcasted_iota(jnp.int32, (cap, rows), 0).astype(jnp.float32)
+    flat[...] = jnp.zeros_like(flat)
+    wanted = flip(routes_ref[...].astype(jnp.float32))
+    named = lax.broadcasted_iota(jnp.int32, (n_exp, rows), 0).astype(jnp.float32)
+    hits = wanted[0:1] == named
+    for k in range(1, routes_ref.shape[1]):
+        hits = hits | (wanted[k : k + 1] == named)
+    early = lax.broadcasted_iota(jnp.int32, (rows, rows), 0)
+    late = lax.broadcasted_iota(jnp.int32, (rows, rows), 1)
+    before = jnp.where(early < late, 1.0, 0.0).astype(jnp.bfloat16)
+    marks = jnp.where(hits, 1.0, 0.0)
+    ranks = jnp.dot(marks.astype(jnp.bfloat16), before, preferred_element_type=jnp.float32)
+    places[...] = jnp.where(hits, ranks, -1.0)
+
+    widened = residual_ref[...].astype(jnp.float32)
+    inv_rms = lax.rsqrt(jnp.mean(widened * widened, axis=1, keepdims=True) + eps)
+    ffn_ref[...] = (widened * inv_rms * gain_ref[...][None, :]).astype(jnp.bfloat16)
 
     def transfer(src, dst, send, recv, e, pos, piece, peer):
         part = pl.ds(piece * PIECE, PIECE)
@@ -422,7 +472,10 @@
         )
 
     def pack(e):
-        pick = jnp.concatenate([map_ref[owner, e] for owner in owners], axis=0)
+        pick = jnp.concatenate(
+            [jnp.where(row == count, 1.0, 0.0).astype(jnp.bfloat16) for row in spread(places, e)],
+            axis=0,
+        )
 
         @pl.loop(0, columns // tile)
         def _(j):
@@ -477,12 +530,35 @@
     pl.semaphore_wait(barrier, n_dp - 1)
     dispatch(0)
     pack(1)
+    logits = flip(jnp.dot(ffn_ref[...], router_ref[...], preferred_element_type=jnp.float32))
+    dispatch(1)
+    peak = jnp.max(jnp.where(hits, logits, neg_fill), axis=0, keepdims=True)
+    expl = jnp.where(hits, jnp.exp(jnp.where(hits, logits, peak) - peak), 0.0)
+    shares = expl / jnp.sum(expl, axis=0, keepdims=True)
+    high[...] = shares.astype(jnp.bfloat16).astype(jnp.float32)
+    rest[...] = shares - high[...]
     for e in range(n_local):
-        for i, ref in enumerate((back_ref, rest_ref)):
-            joined = jnp.concatenate([ref[owner, e] for owner in owners], axis=0)
-            back[e, i] = joined.T
-        if e == 0:
-            dispatch(1)
+        chosen = [row == count for row in spread(places, e)]
+        for i, table in enumerate((high, rest)):
+            joined = jnp.concatenate(
+                [jnp.where(c, row, 0.0) for c, row in zip(chosen, spread(table, e))], axis=0
+            )
+            back[e, i] = joined.T.astype(jnp.bfloat16)
+
+    kv_copy.wait()
+    held = pool_ref.shape[0]
+    for i in range(held):
+        mine = lax.axis_index("mp") * held + i
+
+        def pick_page(p, page):
+            here = page_slots_ref[pl.ds(p, 1), 0:1] == mine
+            return jnp.where(here, pages[p].astype(jnp.float32), page)
+
+        page = lax.fori_loop(
+            0, pages.shape[0], pick_page, jnp.zeros(pages.shape[1:], jnp.float32)
+        )
+        pool_ref[i] = page.astype(jnp.bfloat16)
+
     up_copy.wait()
     down_copy.wait()
     for e in range(n_local):
@@ -497,20 +573,25 @@
         whole(produced, returned, back_send, back_recv, e).wait_send()
 
 
-def experts(ffn_in, send_map, back_high, back_rest, residual, gate_up_weight, down_weight):
-    rows, columns = ffn_in.shape
+def experts(
+    residual, gain, router, routes, page_slots, group_kv, held, gate_up_weight, down_weight
+):
+    rows, columns = residual.shape
     n_dp = lax.axis_size("dp")
     n_local, hidden = down_weight.shape[:2]
+    n_exp = router.shape[1]
     dma = pltpu.SemaphoreType.DMA
     vmem = pl.BlockSpec(memory_space=pltpu.VMEM)
     hbm = pl.BlockSpec(memory_space=pl.ANY)
     block = (n_local, n_dp, CAP, columns)
-    maps = [m.reshape(n_dp, n_local, CAP, rows) for m in (send_map, back_high, back_rest)]
     return pl.pallas_call(
         expert_kernel,
-        in_specs=[vmem] * 5 + [hbm] * 2,
-        out_specs=vmem,
-        out_shape=jax.ShapeDtypeStruct((rows, columns), jnp.bfloat16),
+        in_specs=[vmem] * 5 + [hbm] * 3,
+        out_specs=[vmem] * 2,
+        out_shape=[
+            jax.ShapeDtypeStruct((rows, columns), jnp.bfloat16),
+            jax.ShapeDtypeStruct((held,) + group_kv.shape[1:], jnp.bfloat16),
+        ],
         scratch_shapes=[
             pltpu.VMEM(block, jnp.bfloat16),
             pltpu.VMEM(block, jnp.bfloat16),
@@ -521,17 +602,23 @@
             pltpu.VMEM((n_dp * CAP, hidden), jnp.bfloat16),
             pltpu.VMEM((n_local, 2, rows, n_dp * CAP), jnp.bfloat16),
             pltpu.VMEM((rows, columns), jnp.float32),
+            pltpu.VMEM((rows, columns), jnp.bfloat16),
+            pltpu.VMEM(group_kv.shape, jnp.bfloat16),
+            pltpu.VMEM((rows, 128), jnp.float32),
+            pltpu.VMEM((n_exp, rows), jnp.float32),
+            pltpu.VMEM((n_exp, rows), jnp.float32),
+            pltpu.VMEM((n_exp, rows), jnp.float32),
             dma((n_local,)),
             dma((n_local,)),
             dma((n_local,)),
             dma((n_local,)),
-            dma((2,)),
+            dma((3,)),
         ],
         compiler_params=pltpu.CompilerParams(
             collective_id=1, has_side_effects=True, vmem_limit_bytes=60 << 20
         ),
         name="experts",
-    )(ffn_in, *maps, residual, gate_up_weight, down_weight)
+    )(residual, gain, router, routes, page_slots, group_kv, gate_up_weight, down_weight)
 
 
 def shards(
@@ -550,69 +637,27 @@
     expert_gate_up_weight,
     expert_down_weight,
 ):
-    tokens_per_shard, model_columns = tokens.shape
-    mp_index = lax.axis_index("mp")
-    group_start = mp_index * tokens_per_shard
-    n_exp = router.shape[1]
-
-    packed = jnp.concatenate([adapter_down_weight[0].T, adapter_up_weight[0]], axis=0)
-
-    seq_ends = jnp.sum(
-        jnp.where(
-            jnp.arange(lengths.shape[1])[:, None] <= jnp.arange(lengths.shape[1])[None, :],
-            lengths[0][:, None],
-            0,
-        ),
-        axis=0,
-    )
-    positions = group_start + jnp.arange(tokens_per_shard, dtype=jnp.int32)
-    passed = positions[:, None] >= seq_ends[None, :]
-    query_seg = jnp.sum(passed.astype(jnp.int32), axis=1)
-    low = jnp.max(jnp.where(passed, seq_ends[None, :], 0), axis=1, keepdims=True)
-    seq_match = query_seg[:, None] == jnp.arange(lengths.shape[1], dtype=jnp.int32)[None, :]
-    token_adapter = jnp.sum(jnp.where(seq_match, request_adapter[0][None, :], 0), axis=1)
-
     residual, group_kv = front(
         tokens,
-        attention_gain[None, :],
+        attention_gain,
         query_key_value_weight,
-        packed,
-        token_adapter[:, None],
-        low,
+        adapter_down_weight,
+        adapter_up_weight,
+        lengths,
+        request_adapter,
         output_weight.T,
     )
-
-    pages_dev = tokens_per_shard // PAGE
     pages_grp = group_page_slots.shape[1]
-    my_slots = mp_index * pages_dev + jnp.arange(pages_dev, dtype=jnp.int32)
-    slot_match = (group_page_slots[0][None, :] == my_slots[:, None]).astype(jnp.int32)
-    source_page = jnp.sum(slot_match * jnp.arange(pages_grp, dtype=jnp.int32)[None, :], axis=1)
-    pages = group_kv.reshape(pages_grp, PAGE, group_kv.shape[2])
-    pool = jnp.concatenate(
-        [lax.dynamic_slice_in_dim(pages, source_page[i], 1, axis=0) for i in range(pages_dev)], axis=0
-    )
-
-    ffn_in = rms_norm(residual, expert_norm_gain)
-    logits = jnp.dot(ffn_in, router, preferred_element_type=jnp.float32)
-    hits = jnp.any(routes[:, :, None] == jnp.arange(n_exp, dtype=jnp.int32)[None, None, :], axis=1)
-    peak = jnp.max(jnp.where(hits, logits, neg_fill), axis=1, keepdims=True)
-    expl = jnp.where(hits, jnp.exp(jnp.where(hits, logits, peak) - peak), 0.0)
-    route_weights = expl / jnp.sum(expl, axis=1, keepdims=True)
-    before = (
-        jnp.arange(tokens_per_shard)[None, :] < jnp.arange(tokens_per_shard)[:, None]
-    ).astype(jnp.bfloat16)
-    place = jnp.dot(before, hits.astype(jnp.bfloat16), preferred_element_type=jnp.float32)
-    place = jnp.where(hits, place, -1.0).T
-    chosen = place[:, None, :] == jnp.arange(CAP, dtype=jnp.int32).astype(jnp.float32)[None, :, None]
-    send_map = chosen.astype(jnp.bfloat16).reshape(n_exp * CAP, tokens_per_shard)
-    high = route_weights.astype(jnp.bfloat16)
-    rest = (route_weights - high.astype(jnp.float32)).astype(jnp.bfloat16)
-    zero = jnp.zeros((), jnp.bfloat16)
-    back_high = jnp.where(chosen, high.T[:, None, :], zero).reshape(n_exp * CAP, tokens_per_shard)
-    back_rest = jnp.where(chosen, rest.T[:, None, :], zero).reshape(n_exp * CAP, tokens_per_shard)
-
-    layer_out = experts(
-        ffn_in, send_map, back_high, back_rest, residual, expert_gate_up_weight, expert_down_weight
+    layer_out, pool = experts(
+        residual,
+        expert_norm_gain,
+        router,
+        routes,
+        group_page_slots.reshape(pages_grp, 1),
+        group_kv.reshape(pages_grp, PAGE, group_kv.shape[2]),
+        tokens.shape[0] // PAGE,
+        expert_gate_up_weight,
+        expert_down_weight,
     )
     return (layer_out, pool)
 

time: 207 us -> 196 us (0.947)
  other arithmetic: 8.46 us -> 0 us
  between operations: 4.63 us -> 0.65 us
  local copies, waits for them, and re-layouts: 6.71 us -> 10.1 us
    unnamed x9 -> x5, local copies, waits for them, and re-layouts: 2.09 us -> 8.74 us
    broadcast_in_dim x5 -> x0, local copies, waits for them, and re-layouts: 2.93 us -> none  [the longest x1 1.3 us: shards(): attention_gain[None, :]]
    reduce_sum x5 -> x0, other arithmetic: 2.62 us -> none  [the longest x1 0.87 us: shards(): jnp.sum(slot_match * jnp.arange(pages_grp, dtype=jnp.int32)[None, :], axi...]
    concatenate x2 -> x0, other arithmetic: 2.18 us -> none  [the longest x1 1.46 us: shards(): jnp.concatenate([adapter_down_weight[0].T, adapter_up_weight[0]], axis=0)]
where the time goes in v4:
time: 196 us; the launch traced here: 195 us
  Pallas kernels  184 us (94%)
  local copies, waits for them, and re-layouts  10.1 us (5%)
    pallas_call x1, Pallas kernels, experts(): pl.pallas_call(expert_kernel, in_specs=[vmem] * 5 + [hbm] * 3, out_specs=...  111 us
    pallas_call x1, Pallas kernels, front(): pl.pallas_call(front_kernel, in_specs=[vmem] * 8, out_specs=[vmem] * 2, o...  73.1 us
    unnamed x5, local copies, waits for them, and re-layouts  8.74 us

profile of v4, /device:TPU:6, one launch (start us, length us, event | category | flops | bytes accessed | tf_op | source)
XLA Modules:
  0.0 194.7 jit_solution(7343921874118458349)
XLA Ops:
  0.6 1.3 copy.19.page_slots_ref
  2.0 1.5 copy.18.routes_ref
  3.4 1.7 copy.16.down_ref
  5.2 1.8 copy.17.router_ref
  7.0 73.1 %front.1 = (bf16[256,1536]{1,0:T(8,128)(2,1)}, bf16[8,256,512]{2,1,0:T(8,128)(2,1)}) custom-call(bf16[256,1536]{1,0:T(8,128)(2,1)} %tokens_ref.1, f32[1536]{0:T(1024)} %gain_ref.2, bf16[1536,256]{1,0:T(8,128)(2,1)} %weight_ref.1, bf16[1,1536,16]{2,1,0:T(8,128)(2,1)} %copy.16.down_ref, bf16[1,16,1536]{2,1,0:T(8,128)(2,1)} %up_ref.1, s32[1,4]{1,0:T(1,128)} %lengths_ref.1, ...), custom_call_target="tpu_custom_call" | custom-call | tf_op jit(solution)/shard_map/front/pallas_call | solution.py:319
  80.1 110.9 %experts.1 = (bf16[256,1536]{1,0:T(8,128)(2,1)}, bf16[2,128,512]{2,1,0:T(8,128)(2,1)}) custom-call(bf16[256,1536]{1,0:T(8,128)(2,1)} %get-tuple-element.4.residual_ref, f32[1536]{0:T(1024)} %gain_ref.3, bf16[1536,32]{1,0:T(8,128)(2,1)} %copy.17.router_ref, s32[256,4]{1,0:T(8,128)} %copy.18.routes_ref, s32[16,1]{1,0:T(8,128)} %copy.19.page_slots_ref, ...), custom_call_target="tpu_custom_call" | custom-call | tf_op jit(solution)/shard_map/experts/pallas_call | solution.py:587
  191.0 2.1 %copy.22 = bf16[256,1536]{1,0:T(8,128)(2,1)} copy(bf16[256,1536]{1,0:T(8,128)(2,1)} %get-tuple-element.8) | data formatting | bytes 1572864
  193.0 1.7 copy.23

commit v5 on v4

--- a/solution.py
+++ b/solution.py
@@ -18,7 +18,7 @@
 
 
 class Ring:
-    def __init__(self, buf, own, send, recv):
+    def __init__(self, buf, own, send, recv, span):
         me = lax.axis_index("mp")
         n = lax.axis_size("mp")
         chips = n // 2
@@ -29,7 +29,7 @@
         self.me = me
         self.partner = x * 2 + 1 - core
         self.buf, self.own, self.send, self.recv = buf, own, send, recv
-        self.half = buf.shape[1] // 2
+        self.half = span // 2
 
     def other(self, slot):
         return slot + 1 - 2 * lax.rem(slot, 2)
@@ -97,6 +97,120 @@
 
 
 HOPS = 14
+SIDE = 4
+
+
+class Spread:
+    def __init__(self, ring, buf, own, base, send, recv):
+        dp = lax.axis_index("dp")
+        self.index = (dp // SIDE, lax.rem(dp, SIDE))
+        self.ring, self.buf, self.own, self.base = ring, buf, own, base
+        self.chunk = (buf.shape[1] - base) // SIDE
+        self.wide = buf.shape[2] // 2
+        self.send, self.recv = send, recv
+        self.slots = (ring.left, ring.right, ring.far)
+
+    def piece(self, ref, part, index):
+        rows = pl.ds(self.base + index * self.chunk, self.chunk)
+        return ref.at[rows, pl.ds(part * self.wide, self.wide)]
+
+    def across(self, i, slot, part, target, own=False):
+        index = self.index[part]
+        return pltpu.make_async_remote_copy(
+            src_ref=self.piece(self.own if own else self.buf.at[slot], part, index),
+            dst_ref=self.piece(self.buf.at[slot], part, index),
+            send_sem=self.send.at[i],
+            recv_sem=self.recv.at[i],
+            device_id={"mp": target},
+            device_id_type=MESH,
+        )
+
+    def along(self, s, part, d, back=False):
+        z, y = self.index
+        step = SIDE - d if back else d
+        peer = (
+            lax.rem(z + step, SIDE) * SIDE + y if part == 0 else z * SIDE + lax.rem(y + step, SIDE)
+        )
+        index = lax.rem(self.index[part] + step, SIDE) if back else self.index[part]
+        ref = self.piece(self.buf.at[self.slots[s]], part, index)
+        i = 6 + (s * 2 + part) * 3 + d - 1
+        return pltpu.make_async_remote_copy(
+            src_ref=ref,
+            dst_ref=ref,
+            send_sem=self.send.at[i],
+            recv_sem=self.recv.at[i],
+            device_id={"dp": peer},
+            device_id_type=MESH,
+        )
+
+    def hand(self, i, slot, own=False):
+        rows = pl.ds(self.base, SIDE * self.chunk)
+        return pltpu.make_async_remote_copy(
+            src_ref=self.own.at[rows] if own else self.buf.at[slot, rows],
+            dst_ref=self.buf.at[slot, rows],
+            send_sem=self.send.at[i],
+            recv_sem=self.recv.at[i],
+            device_id={"mp": self.ring.partner},
+            device_id_type=MESH,
+        )
+
+    def begin(self):
+        ring = self.ring
+        self.across(0, ring.me, 0, ring.right, True).start()
+        self.across(1, ring.me, 1, ring.left, True).start()
+        self.across(2, ring.me, 1, ring.right, True).start()
+        self.across(3, ring.me, 0, ring.left, True).start()
+        self.hand(27, ring.me, True).start()
+
+    def push(self, s, part):
+        for d in (2, 1, 3):
+            self.along(s, part, d).start()
+
+    def near(self):
+        ring = self.ring
+        self.across(0, ring.left, 0, ring.right).wait_recv()
+        self.across(4, ring.left, 0, ring.right).start()
+        self.push(0, 0)
+        self.across(1, ring.right, 1, ring.left).wait_recv()
+        self.across(5, ring.right, 1, ring.left).start()
+        self.push(1, 1)
+        self.across(2, ring.left, 1, ring.right).wait_recv()
+        self.push(0, 1)
+        self.across(3, ring.right, 0, ring.left).wait_recv()
+        self.push(1, 0)
+
+    def distant(self):
+        ring = self.ring
+        self.across(4, ring.far, 0, ring.right).wait_recv()
+        self.push(2, 0)
+        self.across(5, ring.far, 1, ring.left).wait_recv()
+        self.push(2, 1)
+
+    def finish(self, s):
+        for part in (0, 1):
+            for d in (1, 2, 3):
+                self.along(s, part, d, True).wait_recv()
+        self.hand(24 + s, self.slots[s]).start()
+
+    def got(self, s):
+        self.hand(24 + s, self.ring.other(self.slots[s])).wait_recv()
+
+    def got_partner(self):
+        self.hand(27, self.ring.partner).wait_recv()
+
+    def drain(self):
+        ring = self.ring
+        for i in range(6):
+            self.across(i, ring.me, (0, 1, 1, 0, 0, 1)[i], ring.right, True).wait_send()
+        for s in range(3):
+            for part in (0, 1):
+                for d in (1, 2, 3):
+                    self.along(s, part, d).wait_send()
+            self.hand(24 + s, self.slots[s]).wait_send()
+        self.hand(27, ring.me, True).wait_send()
+
+
+PASSES = 28
 
 
 def front_kernel(
@@ -122,12 +236,15 @@
     packed_ref,
     weight_send,
     weight_recv,
+    low_send,
+    low_recv,
     kv_send,
     kv_recv,
     out_send,
     out_recv,
     adapter_send,
     adapter_recv,
+    pair_sem,
     local_sem,
 ):
     dp, mp = lax.axis_index("dp"), lax.axis_index("mp")
@@ -138,9 +255,12 @@
     q_blocks = qkv.shape[0] - 2
     rank = up_ref.shape[1]
 
-    ring = Ring(weights, weight_ref, weight_send, weight_recv)
-    kv_ring = Ring(kv_ref, kv_ref.at[mp], kv_send, kv_recv)
-    out_ring = Ring(out_weights, out_weight_ref, out_send, out_recv)
+    depth = weight_ref.shape[0]
+    core = lax.rem(mp, 2)
+    ring = Ring(weights, weight_ref, weight_send, weight_recv, depth // 2)
+    low_rows = Spread(ring, weights, weight_ref, depth // 2, low_send, low_recv)
+    kv_ring = Ring(kv_ref, kv_ref.at[mp], kv_send, kv_recv, rows)
+    out_rows = Spread(ring, out_weights, out_weight_ref, 0, out_send, out_recv)
 
     barrier = pltpu.get_barrier_semaphore()
     for peer in (ring.left, ring.right, ring.partner):
@@ -155,31 +275,42 @@
 
     def adapter_copy(k, slot, peer):
         return pltpu.make_async_remote_copy(
-            src_ref=packed_ref,
-            dst_ref=adapters.at[slot],
+            src_ref=packed_ref.at[core],
+            dst_ref=adapters.at[core, slot],
             send_sem=adapter_send.at[k],
             recv_sem=adapter_recv.at[slot],
             device_id={"dp": peer},
             device_id_type=MESH,
         )
 
+    def adapter_pair(kind):
+        return pltpu.make_async_remote_copy(
+            src_ref=adapters.at[kind],
+            dst_ref=adapters.at[kind],
+            send_sem=pair_sem.at[0],
+            recv_sem=pair_sem.at[1],
+            device_id={"mp": ring.partner},
+            device_id_type=MESH,
+        )
+
+    low_rows.begin()
     ring.begin()
 
-    packed_ref[rank:, :] = up_ref[0]
-    packed_ref[:rank, :] = down_ref[0].astype(jnp.float32).T.astype(jnp.bfloat16)
-
+    packed_ref[0] = down_ref[0]
+    packed_ref[1] = up_ref[0]
     own_out = pltpu.make_async_copy(out_weight_ref, out_weights.at[mp], local_sem)
     own_out.start()
 
     widened = tokens_ref[...].astype(jnp.float32)
     inv_rms = lax.rsqrt(jnp.mean(widened * widened, axis=1, keepdims=True) + eps)
     normed[...] = (widened * inv_rms * gain_ref[...][None, :]).astype(jnp.bfloat16)
+    adapters[core, dp] = packed_ref[core]
+
+    low_rows.near()
 
     @pl.loop(1, n_dp)
     def _(k):
         adapter_copy(k, dp, lax.rem(dp + k, n_dp)).start()
-
-    adapters[dp] = packed_ref[...]
 
     place = lax.broadcasted_iota(jnp.int32, (rows, 1), 0) + mp * rows
     low = jnp.zeros((rows, 1), jnp.int32)
@@ -200,49 +331,62 @@
         qkv[slot] = jnp.dot(normed[...], weights[slot], preferred_element_type=jnp.float32)
 
     qkv[mp] = jnp.dot(normed[...], weight_ref[...], preferred_element_type=jnp.float32)
+    low_rows.distant()
+    ring.forward_near()
     ring.got_partner()
+    low_rows.got_partner()
     project(ring.partner)
-    ring.forward_near()
+    low_rows.finish(0)
+    low_rows.finish(1)
     ring.forward_rest()
     project(ring.left)
     project(ring.right)
+    low_rows.finish(2)
+    ring.forward_far()
+    out_rows.begin()
+    project(ring.far)
+    ring.got_near()
+    low_rows.got(0)
+    low_rows.got(1)
+    project(ring.other(ring.left))
+    project(ring.other(ring.right))
+    ring.got_far()
+    low_rows.got(2)
+    project(ring.other(ring.far))
+
+    kv_ref[mp, :, :wide] = qkv[q_blocks].astype(jnp.bfloat16)
+    kv_ref[mp, :, wide:] = qkv[q_blocks + 1].astype(jnp.bfloat16)
 
     @pl.loop(1, n_dp)
     def _(k):
         source = lax.rem(dp + k, n_dp)
         adapter_copy(k, source, source).wait_recv()
 
-    down = adapters[:, :rank, :].reshape(n_dp * rank, columns)
+    adapter_pair(core).start()
+    kv_ring.begin()
+    adapter_pair(1 - core).wait_recv()
+
+    down = adapters[0].reshape(n_dp * rank, columns)
     mid = lax.dot_general(
         normed[...], down, (((1,), (1,)), ((), ())), preferred_element_type=jnp.float32
     )
     owner = lax.broadcasted_iota(jnp.int32, (rows, n_dp * rank), 1) // rank
     middle[...] = jnp.where(owner == adapter, mid, 0.0).astype(jnp.bfloat16)
 
-    ring.got_near()
-    project(ring.other(ring.left))
-    project(ring.other(ring.right))
-    ring.forward_far()
-    project(ring.far)
-    ring.got_far()
-    project(ring.other(ring.far))
-
-    kv_ref[mp, :, :wide] = qkv[q_blocks].astype(jnp.bfloat16)
-    kv_ref[mp, :, wide:] = qkv[q_blocks + 1].astype(jnp.bfloat16)
-
     def finish_query(j):
-        up = adapters[:, rank:, j * wide : (j + 1) * wide].reshape(n_dp * rank, wide)
+        up = adapters[1, :, :, j * wide : (j + 1) * wide].reshape(n_dp * rank, wide)
         extra = jnp.dot(middle[...], up, preferred_element_type=jnp.float32)
         query[j] = (qkv[j] + extra).astype(jnp.bfloat16)
 
     finish_query(0)
-    kv_ring.begin()
-    for j in range(1, q_blocks):
+    finish_query(1)
+    out_rows.near()
+    kv_ring.forward_near()
+    for j in range(2, q_blocks):
         finish_query(j)
-    kv_ring.forward_near()
-    out_ring.begin()
     kv_ring.got_partner()
     kv_ring.forward_rest()
+    out_rows.distant()
     kv_ring.got_near()
     kv_ring.forward_far()
     kv_ring.got_far()
@@ -276,13 +420,13 @@
                 attended[block, :, cols] = (mixed / total).astype(jnp.bfloat16)
 
         if kv_head == 0:
-            out_ring.forward_near()
-
-    out_ring.forward_rest()
-    out_ring.got_partner()
-    out_ring.got_near()
-    out_ring.forward_far()
-    out_ring.got_far()
+            out_rows.finish(0)
+            out_rows.finish(1)
+
+    out_rows.finish(2)
+    out_rows.got_partner()
+    for s in range(3):
+        out_rows.got(s)
     own_out.wait()
 
     own_rows = out_weights.shape[1]
@@ -300,7 +444,9 @@
 
     ring.drain()
     kv_ring.drain()
-    out_ring.drain()
+    out_rows.drain()
+    low_rows.drain()
+    adapter_pair(core).wait_send()
 
     @pl.loop(1, n_dp)
     def _(k):
@@ -326,7 +472,7 @@
         ],
         scratch_shapes=[
             pltpu.VMEM((n_mp, depth, wide), jnp.bfloat16),
-            pltpu.VMEM((n_dp, 2 * rank, columns), jnp.bfloat16),
+            pltpu.VMEM((2, n_dp, rank, columns), jnp.bfloat16),
             pltpu.VMEM((n_mp,) + out_weight.shape, jnp.bfloat16),
             pltpu.VMEM((n_mp, rows, wide), jnp.float32),
             pltpu.VMEM((q_blocks, rows, wide), jnp.bfloat16),
@@ -334,15 +480,18 @@
             pltpu.VMEM((rows, window), jnp.float32),
             pltpu.VMEM((rows, columns), jnp.bfloat16),
             pltpu.VMEM((rows, n_dp * rank), jnp.bfloat16),
-            pltpu.VMEM((2 * rank, columns), jnp.bfloat16),
+            pltpu.VMEM((2, rank, columns), jnp.bfloat16),
             dma((HOPS,)),
             dma((HOPS,)),
+            dma((PASSES,)),
+            dma((PASSES,)),
             dma((HOPS,)),
             dma((HOPS,)),
-            dma((HOPS,)),
-            dma((HOPS,)),
+            dma((PASSES,)),
+            dma((PASSES,)),
             dma((n_dp,)),
             dma((n_dp,)),
+            dma((2,)),
             dma(()),
         ],
         compiler_params=pltpu.CompilerParams(
@@ -378,7 +527,6 @@
     total,
     ffn_ref,
     pages,
-    flat,
     places,
     high,
     rest,
@@ -422,10 +570,6 @@
     down_copy.start()
     kv_copy.start()
 
-    def flip(values):
-        flat[:, : values.shape[1]] = values
-        return flat[...].T[: values.shape[1]]
-
     def spread(table, e):
         return [
             jnp.broadcast_to(table[pl.ds(owner * n_local + e, 1), :], (cap, rows))
@@ -433,11 +577,10 @@
         ]
 
     count = lax.broadcasted_iota(jnp.int32, (cap, rows), 0).astype(jnp.float32)
-    flat[...] = jnp.zeros_like(flat)
-    wanted = flip(routes_ref[...].astype(jnp.float32))
-    named = lax.broadcasted_iota(jnp.int32, (n_exp, rows), 0).astype(jnp.float32)
+    wanted = routes_ref[...]
+    named = lax.broadcasted_iota(jnp.int32, (n_exp, rows), 0)
     hits = wanted[0:1] == named
-    for k in range(1, routes_ref.shape[1]):
+    for k in range(1, routes_ref.shape[0]):
         hits = hits | (wanted[k : k + 1] == named)
     early = lax.broadcasted_iota(jnp.int32, (rows, rows), 0)
     late = lax.broadcasted_iota(jnp.int32, (rows, rows), 1)
@@ -530,7 +673,9 @@
     pl.semaphore_wait(barrier, n_dp - 1)
     dispatch(0)
     pack(1)
-    logits = flip(jnp.dot(ffn_ref[...], router_ref[...], preferred_element_type=jnp.float32))
+    logits = lax.dot_general(
+        router_ref[...], ffn_ref[...], (((1,), (1,)), ((), ())), preferred_element_type=jnp.float32
+    )
     dispatch(1)
     peak = jnp.max(jnp.where(hits, logits, neg_fill), axis=0, keepdims=True)
     expl = jnp.where(hits, jnp.exp(jnp.where(hits, logits, peak) - peak), 0.0)
@@ -547,11 +692,13 @@
 
     kv_copy.wait()
     held = pool_ref.shape[0]
+    order = lax.broadcasted_iota(jnp.int32, page_slots_ref.shape, 1)
     for i in range(held):
         mine = lax.axis_index("mp") * held + i
 
         def pick_page(p, page):
-            here = page_slots_ref[pl.ds(p, 1), 0:1] == mine
+            slot = jnp.sum(jnp.where(order == p, page_slots_ref[...], 0), axis=1, keepdims=True)
+            here = slot == mine
             return jnp.where(here, pages[p].astype(jnp.float32), page)
 
         page = lax.fori_loop(
@@ -579,7 +726,7 @@
     rows, columns = residual.shape
     n_dp = lax.axis_size("dp")
     n_local, hidden = down_weight.shape[:2]
-    n_exp = router.shape[1]
+    n_exp = router.shape[0]
     dma = pltpu.SemaphoreType.DMA
     vmem = pl.BlockSpec(memory_space=pltpu.VMEM)
     hbm = pl.BlockSpec(memory_space=pl.ANY)
@@ -604,7 +751,6 @@
             pltpu.VMEM((rows, columns), jnp.float32),
             pltpu.VMEM((rows, columns), jnp.bfloat16),
             pltpu.VMEM(group_kv.shape, jnp.bfloat16),
-            pltpu.VMEM((rows, 128), jnp.float32),
             pltpu.VMEM((n_exp, rows), jnp.float32),
             pltpu.VMEM((n_exp, rows), jnp.float32),
             pltpu.VMEM((n_exp, rows), jnp.float32),
@@ -641,7 +787,7 @@
         tokens,
         attention_gain,
         query_key_value_weight,
-        adapter_down_weight,
+        adapter_down_weight.transpose(0, 2, 1),
         adapter_up_weight,
         lengths,
         request_adapter,
@@ -651,9 +797,9 @@
     layer_out, pool = experts(
         residual,
         expert_norm_gain,
-        router,
-        routes,
-        group_page_slots.reshape(pages_grp, 1),
+        router.T,
+        routes.T,
+        group_page_slots,
         group_kv.reshape(pages_grp, PAGE, group_kv.shape[2]),
         tokens.shape[0] // PAGE,
         expert_gate_up_weight,

time: 196 us -> 177 us (0.903)
  Pallas kernels: 184 us -> 171 us
  local copies, waits for them, and re-layouts: 10.1 us -> 3.73 us
    pallas_call x1, Pallas kernels: 73.1 us -> 60.1 us  [front(): pl.pallas_call(front_kernel, in_specs=[vmem] * 8, out_specs=[vmem] * 2, o...]
    unnamed x5 -> x2, local copies, waits for them, and re-layouts: 8.74 us -> 3.73 us
where the time goes in v5:
time: 177 us; the launch traced here: 176 us
  Pallas kernels  171 us (97%)
  local copies, waits for them, and re-layouts  3.73 us (2%)
    pallas_call x1, Pallas kernels, experts(): pl.pallas_call(expert_kernel, in_specs=[vmem] * 5 + [hbm] * 3, out_specs=...  111 us
    pallas_call x1, Pallas kernels, front(): pl.pallas_call(front_kernel, in_specs=[vmem] * 8, out_specs=[vmem] * 2, o...  60.1 us
    unnamed x2, local copies, waits for them, and re-layouts  3.73 us

profile of v5, /device:TPU:6, one launch (start us, length us, event | category | flops | bytes accessed | tf_op | source)
XLA Modules:
  0.0 175.8 jit_solution(4556581330523706610)
XLA Ops:
  0.6 60.1 %front.1 = (bf16[256,1536]{1,0:T(8,128)(2,1)}, bf16[8,256,512]{2,1,0:T(8,128)(2,1)}) custom-call(bf16[256,1536]{1,0:T(8,128)(2,1)} %tokens_ref.1, f32[1536]{0:T(1024)} %gain_ref.2, bf16[1536,256]{1,0:T(8,128)(2,1)} %weight_ref.1, bf16[1,16,1536]{2,1,0:T(8,128)(2,1)} %bitcast.8, bf16[1,16,1536]{2,1,0:T(8,128)(2,1)} %up_ref.1, s32[1,4]{1,0:T(1,128)} %lengths_ref.1, ...), custom_call_target="tpu_custom_call" | custom-call | tf_op jit(solution)/shard_map/front/pallas_call | solution.py:465
  60.7 111.4 %experts.1 = (bf16[256,1536]{1,0:T(8,128)(2,1)}, bf16[2,128,512]{2,1,0:T(8,128)(2,1)}) custom-call(bf16[256,1536]{1,0:T(8,128)(2,1)} %get-tuple-element.4.residual_ref, f32[1536]{0:T(1024)} %gain_ref.3, bf16[32,1536]{1,0:T(8,128)(2,1)} %bitcast.7, s32[4,256]{1,0:T(4,128)} %bitcast.9, s32[1,16]{1,0:T(1,128)} %page_slots_ref.1, bf16[16,128,512]{2,1,0:T(8,128)(2,1)} %bitcast.5, ...), custom_call_target="tpu_custom_call" | custom-call | tf_op jit(solution)/shard_map/experts/pallas_call | solution.py:734
  172.1 2.1 %copy.18 = bf16[256,1536]{1,0:T(8,128)(2,1)} copy(bf16[256,1536]{1,0:T(8,128)(2,1)} %get-tuple-element.8) | data formatting | bytes 1572864
  174.2 1.7 copy.19

commit v6 on v5

--- a/solution.py
+++ b/solution.py
@@ -530,6 +530,14 @@
     places,
     high,
     rest,
+    along_z,
+    along_y,
+    places_z,
+    places_y,
+    near_send,
+    near_recv,
+    table_send,
+    table_recv,
     go_send,
     go_recv,
     back_send,
@@ -537,8 +545,9 @@
     local_sem,
 ):
     dp = lax.axis_index("dp")
-    n_local, n_dp, cap, columns = sent.shape
-    side = 4
+    n_local, n_dp, cap, columns = produced.shape
+    side = SIDE
+    half = columns // 2
     z, y = dp // side, lax.rem(dp, side)
     slots = n_dp * cap
     hidden = down.shape[1]
@@ -554,7 +563,10 @@
             lax.rem(z + side - k // side, side) * side + lax.rem(y + side - k % side, side)
         )
 
-    owners = [toward(k) for k in ORDER]
+    def transposed(k):
+        return k % side * side + k // side
+
+    owners = [toward(transposed(pos)) for pos in range(n_dp)]
 
     barrier = pltpu.get_barrier_semaphore()
 
@@ -570,10 +582,10 @@
     down_copy.start()
     kv_copy.start()
 
-    def spread(table, e):
+    def spread(table, e, holders):
         return [
             jnp.broadcast_to(table[pl.ds(owner * n_local + e, 1), :], (cap, rows))
-            for owner in owners
+            for owner in holders
         ]
 
     count = lax.broadcasted_iota(jnp.int32, (cap, rows), 0).astype(jnp.float32)
@@ -588,10 +600,14 @@
     marks = jnp.where(hits, 1.0, 0.0)
     ranks = jnp.dot(marks.astype(jnp.bfloat16), before, preferred_element_type=jnp.float32)
     places[...] = jnp.where(hits, ranks, -1.0)
+    places_z[z] = places[...]
+    places_y[y] = places[...]
 
     widened = residual_ref[...].astype(jnp.float32)
     inv_rms = lax.rsqrt(jnp.mean(widened * widened, axis=1, keepdims=True) + eps)
     ffn_ref[...] = (widened * inv_rms * gain_ref[...][None, :]).astype(jnp.bfloat16)
+    along_z[z] = ffn_ref[:, :half]
+    along_y[y] = ffn_ref[:, half:]
 
     def transfer(src, dst, send, recv, e, pos, piece, peer):
         part = pl.ds(piece * PIECE, PIECE)
@@ -614,32 +630,79 @@
             device_id_type=MESH,
         )
 
-    def pack(e):
+    fields = (along_z, along_y)
+    tables = (places_z, places_y)
+    index = (z, y)
+
+    def peer_at(part, d):
+        if part == 0:
+            return lax.rem(z + d, side) * side + y
+        return z * side + lax.rem(y + d, side)
+
+    def near(ref, send, recv, part, d, back=False):
+        step = side - d if back else 0
+        spot = ref.at[lax.rem(index[part] + step, side)]
+        i = part * (side - 1) + d - 1
+        return pltpu.make_async_remote_copy(
+            src_ref=spot,
+            dst_ref=spot,
+            send_sem=send.at[i],
+            recv_sem=recv.at[i],
+            device_id={"dp": peer_at(part, d)},
+            device_id_type=MESH,
+        )
+
+    def landing(part, e, d, i):
+        if part == 0:
+            return arrived.at[e, d, i, :, pl.ds(0, half)]
+        return arrived.at[e, i, d, :, pl.ds(half, half)]
+
+    def leg(part, e, d, i):
+        sem = (e * 2 + part) * (side - 1) + d - 1
+        return pltpu.make_async_remote_copy(
+            src_ref=sent.at[part, e, d, i],
+            dst_ref=landing(part, e, d, i),
+            send_sem=go_send.at[sem],
+            recv_sem=go_recv.at[sem],
+            device_id={"dp": peer_at(1 - part, d)},
+            device_id_type=MESH,
+        )
+
+    def legs(part, e, d):
+        sem = (e * 2 + part) * (side - 1) + d - 1
+        return pltpu.make_async_remote_copy(
+            src_ref=sent.at[part, e, d],
+            dst_ref=landing(part, e, d, slice(None)),
+            send_sem=go_send.at[sem],
+            recv_sem=go_recv.at[sem],
+            device_id={"dp": peer_at(1 - part, d)},
+            device_id_type=MESH,
+        )
+
+    def pack(part, e, i):
+        origin = lax.rem(index[part] + side - i, side)
+        table = tables[part].at[origin]
         pick = jnp.concatenate(
-            [jnp.where(row == count, 1.0, 0.0).astype(jnp.bfloat16) for row in spread(places, e)],
+            [
+                jnp.where(row == count, 1.0, 0.0).astype(jnp.bfloat16)
+                for row in spread(table, e, [peer_at(1 - part, d) for d in range(side)])
+            ],
             axis=0,
         )
-
-        @pl.loop(0, columns // tile)
-        def _(j):
-            cols = pl.ds(pl.multiple_of(j * tile, tile), tile)
-            got = jnp.dot(pick, ffn_ref[:, cols], preferred_element_type=jnp.float32)
-            sent[e, :, :, cols] = got.astype(jnp.bfloat16).reshape(n_dp, cap, tile)
-
-    def dispatch(e):
-        for piece in range(cap // PIECE):
-            for pos in range(1, n_dp):
-                transfer(sent, arrived, go_send, go_recv, e, pos, piece, owners[pos]).start()
-
-    def give_back(e):
-        for piece in range(cap // PIECE):
-            for pos in range(1, n_dp):
-                peer = source(ORDER[pos])
-                transfer(produced, returned, back_send, back_recv, e, pos, piece, peer).start()
+        got = jnp.dot(pick, fields[part][origin], preferred_element_type=jnp.float32)
+        got = got.astype(jnp.bfloat16).reshape(side, cap, half)
+        if part == 0:
+            arrived[e, 0, i, :, :half] = got[0]
+        else:
+            arrived[e, i, 0, :, half:] = got[0]
+        for d in range(1, side):
+            sent[part, e, d, i] = got[d]
+
+    def dispatch(part, e, i):
+        for d in (2, 1, 3):
+            leg(part, e, d, i).start()
 
     def compute(e):
-        arrived[e, 0] = sent[e, 0]
-
         @pl.loop(0, hidden // 256)
         def _(j):
             gate_cols = pl.ds(pl.multiple_of(j * 256, 256), 256)
@@ -656,6 +719,12 @@
             produced[e, :, :, cols] = made.astype(jnp.bfloat16).reshape(n_dp, cap, 256)
 
         returned[e, 0] = produced[e, 0]
+
+    def give_back(e):
+        for piece in range(cap // PIECE):
+            for k in ORDER[1:]:
+                pos, peer = transposed(k), source(k)
+                transfer(produced, returned, back_send, back_recv, e, pos, piece, peer).start()
 
     def combine(e):
         @pl.loop(0, columns // tile)
@@ -669,24 +738,41 @@
             else:
                 out_ref[:, cols] = (total[:, cols] + mixed).astype(jnp.bfloat16)
 
-    pack(0)
     pl.semaphore_wait(barrier, n_dp - 1)
-    dispatch(0)
-    pack(1)
+    for d in (1, 3, 2):
+        for part in (0, 1):
+            near(tables[part], table_send, table_recv, part, d).start()
+            near(fields[part], near_send, near_recv, part, d).start()
+    pack(0, 0, 0)
+    pack(1, 0, 0)
+    dispatch(0, 0, 0)
+    waiting = (1, 0, 0)
+    for d in (1, 3, 2):
+        for part in (0, 1):
+            near(tables[part], table_send, table_recv, part, d, True).wait_recv()
+            near(fields[part], near_send, near_recv, part, d, True).wait_recv()
+            pack(part, 0, d)
+            dispatch(*waiting)
+            waiting = (part, 0, d)
+    for i in range(side):
+        for part in (0, 1):
+            pack(part, 1, i)
+            dispatch(*waiting)
+            waiting = (part, 1, i)
     logits = lax.dot_general(
         router_ref[...], ffn_ref[...], (((1,), (1,)), ((), ())), preferred_element_type=jnp.float32
     )
-    dispatch(1)
+    dispatch(*waiting)
     peak = jnp.max(jnp.where(hits, logits, neg_fill), axis=0, keepdims=True)
     expl = jnp.where(hits, jnp.exp(jnp.where(hits, logits, peak) - peak), 0.0)
     shares = expl / jnp.sum(expl, axis=0, keepdims=True)
     high[...] = shares.astype(jnp.bfloat16).astype(jnp.float32)
     rest[...] = shares - high[...]
     for e in range(n_local):
-        chosen = [row == count for row in spread(places, e)]
+        chosen = [row == count for row in spread(places, e, owners)]
         for i, table in enumerate((high, rest)):
             joined = jnp.concatenate(
-                [jnp.where(c, row, 0.0) for c, row in zip(chosen, spread(table, e))], axis=0
+                [jnp.where(c, row, 0.0) for c, row in zip(chosen, spread(table, e, owners))], axis=0
             )
             back[e, i] = joined.T.astype(jnp.bfloat16)
 
@@ -709,15 +795,23 @@
     up_copy.wait()
     down_copy.wait()
     for e in range(n_local):
-        whole(sent, arrived, go_send, go_recv, e).wait_recv()
+        for part in (0, 1):
+            for d in range(1, side):
+                legs(part, e, d).wait_recv()
         compute(e)
         give_back(e)
     for e in range(n_local):
         whole(produced, returned, back_send, back_recv, e).wait_recv()
         combine(e)
     for e in range(n_local):
-        whole(sent, arrived, go_send, go_recv, e).wait_send()
+        for part in (0, 1):
+            for d in range(1, side):
+                legs(part, e, d).wait_send()
         whole(produced, returned, back_send, back_recv, e).wait_send()
+    for d in range(1, side):
+        for part in (0, 1):
+            near(tables[part], table_send, table_recv, part, d).wait_send()
+            near(fields[part], near_send, near_recv, part, d).wait_send()
 
 
 def experts(
@@ -740,8 +834,8 @@
             jax.ShapeDtypeStruct((held,) + group_kv.shape[1:], jnp.bfloat16),
         ],
         scratch_shapes=[
-            pltpu.VMEM(block, jnp.bfloat16),
-            pltpu.VMEM(block, jnp.bfloat16),
+            pltpu.VMEM((2, n_local, SIDE, SIDE, CAP, columns // 2), jnp.bfloat16),
+            pltpu.VMEM((n_local, SIDE, SIDE, CAP, columns), jnp.bfloat16),
             pltpu.VMEM(block, jnp.bfloat16),
             pltpu.VMEM(block, jnp.bfloat16),
             pltpu.VMEM(gate_up_weight.shape, jnp.bfloat16),
@@ -754,8 +848,16 @@
             pltpu.VMEM((n_exp, rows), jnp.float32),
             pltpu.VMEM((n_exp, rows), jnp.float32),
             pltpu.VMEM((n_exp, rows), jnp.float32),
-            dma((n_local,)),
-            dma((n_local,)),
+            pltpu.VMEM((SIDE, rows, columns // 2), jnp.bfloat16),
+            pltpu.VMEM((SIDE, rows, columns // 2), jnp.bfloat16),
+            pltpu.VMEM((SIDE, n_exp, rows), jnp.float32),
+            pltpu.VMEM((SIDE, n_exp, rows), jnp.float32),
+            dma((2 * SIDE - 2,)),
+            dma((2 * SIDE - 2,)),
+            dma((2 * SIDE - 2,)),
+            dma((2 * SIDE - 2,)),
+            dma((n_local * (2 * SIDE - 2),)),
+            dma((n_local * (2 * SIDE - 2),)),
             dma((n_local,)),
             dma((n_local,)),
             dma((3,)),

time: 177 us -> 170 us (0.960)
  Pallas kernels: 171 us -> 165 us
    pallas_call x1, Pallas kernels: 111 us -> 105 us  [experts(): pl.pallas_call(expert_kernel, in_specs=[vmem] * 5 + [hbm] * 3, out_specs=...]
where the time goes in v6:
time: 170 us; the launch traced here: 169 us
  Pallas kernels  165 us (97%)
  local copies, waits for them, and re-layouts  3.73 us (2%)
    pallas_call x1, Pallas kernels, experts(): pl.pallas_call(expert_kernel, in_specs=[vmem] * 5 + [hbm] * 3, out_specs=...  105 us
    pallas_call x1, Pallas kernels, front(): pl.pallas_call(front_kernel, in_specs=[vmem] * 8, out_specs=[vmem] * 2, o...  60.1 us
    unnamed x2, local copies, waits for them, and re-layouts  3.73 us

profile of v6, /device:TPU:6, one launch (start us, length us, event | category | flops | bytes accessed | tf_op | source)
XLA Modules:
  0.0 169.4 jit_solution(7420277202268627847)
XLA Ops:
  0.6 60.1 %front.1 = (bf16[256,1536]{1,0:T(8,128)(2,1)}, bf16[8,256,512]{2,1,0:T(8,128)(2,1)}) custom-call(bf16[256,1536]{1,0:T(8,128)(2,1)} %tokens_ref.1, f32[1536]{0:T(1024)} %gain_ref.2, bf16[1536,256]{1,0:T(8,128)(2,1)} %weight_ref.1, bf16[1,16,1536]{2,1,0:T(8,128)(2,1)} %bitcast.8, bf16[1,16,1536]{2,1,0:T(8,128)(2,1)} %up_ref.1, s32[1,4]{1,0:T(1,128)} %lengths_ref.1, ...), custom_call_target="tpu_custom_call" | custom-call | tf_op jit(solution)/shard_map/front/pallas_call | solution.py:465
  60.7 104.9 %experts.1 = (bf16[256,1536]{1,0:T(8,128)(2,1)}, bf16[2,128,512]{2,1,0:T(8,128)(2,1)}) custom-call(bf16[256,1536]{1,0:T(8,128)(2,1)} %get-tuple-element.4.residual_ref, f32[1536]{0:T(1024)} %gain_ref.3, bf16[32,1536]{1,0:T(8,128)(2,1)} %bitcast.7, s32[4,256]{1,0:T(4,128)} %bitcast.9, s32[1,16]{1,0:T(1,128)} %page_slots_ref.1, bf16[16,128,512]{2,1,0:T(8,128)(2,1)} %bitcast.5, ...), custom_call_target="tpu_custom_call" | custom-call | tf_op jit(solution)/shard_map/experts/pallas_call | solution.py:828
  165.6 2.1 %copy.18 = bf16[256,1536]{1,0:T(8,128)(2,1)} copy(bf16[256,1536]{1,0:T(8,128)(2,1)} %get-tuple-element.8) | data formatting | bytes 1572864
  167.7 1.7 copy.19

commit v7 on v6

--- a/solution.py
+++ b/solution.py
@@ -501,10 +501,6 @@
     )(tokens, gain, weight, down, up, lengths, request, out_weight)
 
 
-ORDER = (0, 10, 11, 9, 14, 6, 2, 8, 5, 7, 13, 15, 1, 3, 4, 12)
-PIECE = 16
-
-
 def expert_kernel(
     residual_ref,
     gain_ref,
@@ -519,7 +515,9 @@
     sent,
     arrived,
     produced,
-    returned,
+    middle,
+    folding,
+    folded,
     up,
     down,
     active,
@@ -527,26 +525,29 @@
     total,
     ffn_ref,
     pages,
-    places,
-    high,
-    rest,
     along_z,
     along_y,
     places_z,
     places_y,
+    shares_z,
+    shares_y,
     near_send,
     near_recv,
     table_send,
     table_recv,
+    share_send,
+    share_recv,
     go_send,
     go_recv,
     back_send,
     back_recv,
+    fold_send,
+    fold_recv,
     local_sem,
 ):
     dp = lax.axis_index("dp")
-    n_local, n_dp, cap, columns = produced.shape
-    side = SIDE
+    n_local, side, _, cap, columns = produced.shape
+    n_dp = side * side
     half = columns // 2
     z, y = dp // side, lax.rem(dp, side)
     slots = n_dp * cap
@@ -554,19 +555,6 @@
     rows = ffn_ref.shape[0]
     n_exp = n_local * n_dp
     tile = 512
-
-    def toward(k):
-        return lax.rem(z + k // side, side) * side + lax.rem(y + k % side, side)
-
-    def source(k):
-        return (
-            lax.rem(z + side - k // side, side) * side + lax.rem(y + side - k % side, side)
-        )
-
-    def transposed(k):
-        return k % side * side + k // side
-
-    owners = [toward(transposed(pos)) for pos in range(n_dp)]
 
     barrier = pltpu.get_barrier_semaphore()
 
@@ -599,9 +587,9 @@
     before = jnp.where(early < late, 1.0, 0.0).astype(jnp.bfloat16)
     marks = jnp.where(hits, 1.0, 0.0)
     ranks = jnp.dot(marks.astype(jnp.bfloat16), before, preferred_element_type=jnp.float32)
-    places[...] = jnp.where(hits, ranks, -1.0)
-    places_z[z] = places[...]
-    places_y[y] = places[...]
+    places = jnp.where(hits, ranks, -1.0)
+    places_z[z] = places
+    places_y[y] = places
 
     widened = residual_ref[...].astype(jnp.float32)
     inv_rms = lax.rsqrt(jnp.mean(widened * widened, axis=1, keepdims=True) + eps)
@@ -609,29 +597,9 @@
     along_z[z] = ffn_ref[:, :half]
     along_y[y] = ffn_ref[:, half:]
 
-    def transfer(src, dst, send, recv, e, pos, piece, peer):
-        part = pl.ds(piece * PIECE, PIECE)
-        return pltpu.make_async_remote_copy(
-            src_ref=src.at[e, pos, part],
-            dst_ref=dst.at[e, pos, part],
-            send_sem=send.at[e],
-            recv_sem=recv.at[e],
-            device_id={"dp": peer},
-            device_id_type=MESH,
-        )
-
-    def whole(src, dst, send, recv, e):
-        return pltpu.make_async_remote_copy(
-            src_ref=src.at[e, 1:],
-            dst_ref=dst.at[e, 1:],
-            send_sem=send.at[e],
-            recv_sem=recv.at[e],
-            device_id={"dp": owners[1]},
-            device_id_type=MESH,
-        )
-
     fields = (along_z, along_y)
     tables = (places_z, places_y)
+    weights = (shares_z, shares_y)
     index = (z, y)
 
     def peer_at(part, d):
@@ -716,35 +684,74 @@
         def _(j):
             cols = pl.ds(pl.multiple_of(j * 256, 256), 256)
             made = jnp.dot(active[...], down[e, :, cols], preferred_element_type=jnp.float32)
-            produced[e, :, :, cols] = made.astype(jnp.bfloat16).reshape(n_dp, cap, 256)
-
-        returned[e, 0] = produced[e, 0]
-
-    def give_back(e):
-        for piece in range(cap // PIECE):
-            for k in ORDER[1:]:
-                pos, peer = transposed(k), source(k)
-                transfer(produced, returned, back_send, back_recv, e, pos, piece, peer).start()
-
-    def combine(e):
-        @pl.loop(0, columns // tile)
-        def _(j):
-            cols = pl.ds(pl.multiple_of(j * tile, tile), tile)
-            given = returned[e, :, :, cols].reshape(slots, tile)
-            mixed = jnp.dot(back[e, 0], given, preferred_element_type=jnp.float32)
-            mixed += jnp.dot(back[e, 1], given, preferred_element_type=jnp.float32)
-            if e == 0:
-                total[:, cols] = residual_ref[:, cols].astype(jnp.float32) + mixed
-            else:
-                out_ref[:, cols] = (total[:, cols] + mixed).astype(jnp.bfloat16)
+            produced[e, :, :, :, cols] = made.astype(jnp.bfloat16).reshape(side, side, cap, 256)
+
+        middle[0, e, 0] = produced[e, 0, :, :, :half]
+        middle[1, e, 0] = produced[e, :, 0, :, half:]
+
+    def give_back(part, e, d):
+        if part == 0:
+            made = produced.at[e, d, :, :, pl.ds(0, half)]
+        else:
+            made = produced.at[e, :, d, :, pl.ds(half, half)]
+        sem = (e * 2 + part) * (side - 1) + d - 1
+        return pltpu.make_async_remote_copy(
+            src_ref=made,
+            dst_ref=middle.at[part, e, d],
+            send_sem=back_send.at[sem],
+            recv_sem=back_recv.at[sem],
+            device_id={"dp": peer_at(1 - part, side - d)},
+            device_id_type=MESH,
+        )
+
+    def fold(part, i):
+        sem = part * (side - 1) + i - 1
+        return pltpu.make_async_remote_copy(
+            src_ref=folding.at[part, i],
+            dst_ref=folded.at[part, i],
+            send_sem=fold_send.at[sem],
+            recv_sem=fold_recv.at[sem],
+            device_id={"dp": peer_at(part, side - i)},
+            device_id_type=MESH,
+        )
+
+    def weigh(part, i):
+        origin = lax.rem(index[part] + side - i, side)
+        holders = [peer_at(1 - part, d) for d in range(side)]
+        high, rest = [], []
+        for e in range(n_local):
+            spots = spread(tables[part].at[origin], e, holders)
+            for spot, share in zip(spots, spread(weights[part].at[origin], e, holders)):
+                chosen = jnp.where(spot == count, share, 0.0)
+                top = chosen.astype(jnp.bfloat16).astype(jnp.float32)
+                high.append(top)
+                rest.append(chosen - top)
+        back[part, i, 0] = jnp.concatenate(high, axis=0).T.astype(jnp.bfloat16)
+        back[part, i, 1] = jnp.concatenate(rest, axis=0).T.astype(jnp.bfloat16)
+
+    def partial(part, i):
+        given = middle[part, :, :, i].reshape(n_local * side * cap, half)
+        mixed = jnp.dot(back[part, i, 0], given, preferred_element_type=jnp.float32)
+        return mixed + jnp.dot(back[part, i, 1], given, preferred_element_type=jnp.float32)
 
     pl.semaphore_wait(barrier, n_dp - 1)
     for d in (1, 3, 2):
         for part in (0, 1):
             near(tables[part], table_send, table_recv, part, d).start()
             near(fields[part], near_send, near_recv, part, d).start()
+    logits = lax.dot_general(
+        router_ref[...], ffn_ref[...], (((1,), (1,)), ((), ())), preferred_element_type=jnp.float32
+    )
+    peak = jnp.max(jnp.where(hits, logits, neg_fill), axis=0, keepdims=True)
+    expl = jnp.where(hits, jnp.exp(jnp.where(hits, logits, peak) - peak), 0.0)
+    shares = expl / jnp.sum(expl, axis=0, keepdims=True)
+    shares_z[z] = shares
+    shares_y[y] = shares
     pack(0, 0, 0)
     pack(1, 0, 0)
+    for d in (1, 3, 2):
+        for part in (0, 1):
+            near(weights[part], share_send, share_recv, part, d).start()
     dispatch(0, 0, 0)
     waiting = (1, 0, 0)
     for d in (1, 3, 2):
@@ -759,22 +766,13 @@
             pack(part, 1, i)
             dispatch(*waiting)
             waiting = (part, 1, i)
-    logits = lax.dot_general(
-        router_ref[...], ffn_ref[...], (((1,), (1,)), ((), ())), preferred_element_type=jnp.float32
-    )
+    weigh(0, 0)
     dispatch(*waiting)
-    peak = jnp.max(jnp.where(hits, logits, neg_fill), axis=0, keepdims=True)
-    expl = jnp.where(hits, jnp.exp(jnp.where(hits, logits, peak) - peak), 0.0)
-    shares = expl / jnp.sum(expl, axis=0, keepdims=True)
-    high[...] = shares.astype(jnp.bfloat16).astype(jnp.float32)
-    rest[...] = shares - high[...]
-    for e in range(n_local):
-        chosen = [row == count for row in spread(places, e, owners)]
-        for i, table in enumerate((high, rest)):
-            joined = jnp.concatenate(
-                [jnp.where(c, row, 0.0) for c, row in zip(chosen, spread(table, e, owners))], axis=0
-            )
-            back[e, i] = joined.T.astype(jnp.bfloat16)
+    weigh(1, 0)
+    for d in (1, 3, 2):
+        for part in (0, 1):
+            near(weights[part], share_send, share_recv, part, d, True).wait_recv()
+            weigh(part, d)
 
     kv_copy.wait()
     held = pool_ref.shape[0]
@@ -799,19 +797,43 @@
             for d in range(1, side):
                 legs(part, e, d).wait_recv()
         compute(e)
-        give_back(e)
+        for d in (2, 1, 3):
+            for part in (0, 1):
+                give_back(part, e, d).start()
     for e in range(n_local):
-        whole(produced, returned, back_send, back_recv, e).wait_recv()
-        combine(e)
-    for e in range(n_local):
+        for d in range(1, side):
+            for part in (0, 1):
+                give_back(part, e, d).wait_recv()
+    ready = None
+    for i in (2, 1, 3):
         for part in (0, 1):
-            for d in range(1, side):
-                legs(part, e, d).wait_send()
-        whole(produced, returned, back_send, back_recv, e).wait_send()
-    for d in range(1, side):
-        for part in (0, 1):
+            folding[part, i] = partial(part, i).astype(jnp.bfloat16)
+            if ready:
+                fold(*ready).start()
+            ready = (part, i)
+    for part in (0, 1):
+        cols = pl.ds(part * half, half)
+        total[:, cols] = residual_ref[:, cols].astype(jnp.float32) + partial(part, 0)
+        if ready:
+            fold(*ready).start()
+            ready = None
+    for part in (0, 1):
+        cols = pl.ds(part * half, half)
+        for i in range(1, side):
+            fold(part, i).wait_recv()
+        mixed = total[:, cols]
+        for i in range(1, side):
+            mixed += folded[part, i].astype(jnp.float32)
+        out_ref[:, cols] = mixed.astype(jnp.bfloat16)
+    for part in (0, 1):
+        for d in range(1, side):
             near(tables[part], table_send, table_recv, part, d).wait_send()
             near(fields[part], near_send, near_recv, part, d).wait_send()
+            near(weights[part], share_send, share_recv, part, d).wait_send()
+            fold(part, d).wait_send()
+            for e in range(n_local):
+                legs(part, e, d).wait_send()
+                give_back(part, e, d).wait_send()
 
 
 def experts(
@@ -824,7 +846,6 @@
     dma = pltpu.SemaphoreType.DMA
     vmem = pl.BlockSpec(memory_space=pltpu.VMEM)
     hbm = pl.BlockSpec(memory_space=pl.ANY)
-    block = (n_local, n_dp, CAP, columns)
     return pl.pallas_call(
         expert_kernel,
         in_specs=[vmem] * 5 + [hbm] * 3,
@@ -836,30 +857,35 @@
         scratch_shapes=[
             pltpu.VMEM((2, n_local, SIDE, SIDE, CAP, columns // 2), jnp.bfloat16),
             pltpu.VMEM((n_local, SIDE, SIDE, CAP, columns), jnp.bfloat16),
-            pltpu.VMEM(block, jnp.bfloat16),
-            pltpu.VMEM(block, jnp.bfloat16),
+            pltpu.VMEM((n_local, SIDE, SIDE, CAP, columns), jnp.bfloat16),
+            pltpu.VMEM((2, n_local, SIDE, SIDE, CAP, columns // 2), jnp.bfloat16),
+            pltpu.VMEM((2, SIDE, rows, columns // 2), jnp.bfloat16),
+            pltpu.VMEM((2, SIDE, rows, columns // 2), jnp.bfloat16),
             pltpu.VMEM(gate_up_weight.shape, jnp.bfloat16),
             pltpu.VMEM(down_weight.shape, jnp.bfloat16),
             pltpu.VMEM((n_dp * CAP, hidden), jnp.bfloat16),
-            pltpu.VMEM((n_local, 2, rows, n_dp * CAP), jnp.bfloat16),
+            pltpu.VMEM((2, SIDE, 2, rows, n_local * SIDE * CAP), jnp.bfloat16),
             pltpu.VMEM((rows, columns), jnp.float32),
             pltpu.VMEM((rows, columns), jnp.bfloat16),
             pltpu.VMEM(group_kv.shape, jnp.bfloat16),
-            pltpu.VMEM((n_exp, rows), jnp.float32),
-            pltpu.VMEM((n_exp, rows), jnp.float32),
-            pltpu.VMEM((n_exp, rows), jnp.float32),
             pltpu.VMEM((SIDE, rows, columns // 2), jnp.bfloat16),
             pltpu.VMEM((SIDE, rows, columns // 2), jnp.bfloat16),
+            pltpu.VMEM((SIDE, n_exp, rows), jnp.float32),
+            pltpu.VMEM((SIDE, n_exp, rows), jnp.float32),
             pltpu.VMEM((SIDE, n_exp, rows), jnp.float32),
             pltpu.VMEM((SIDE, n_exp, rows), jnp.float32),
             dma((2 * SIDE - 2,)),
             dma((2 * SIDE - 2,)),
             dma((2 * SIDE - 2,)),
             dma((2 * SIDE - 2,)),
+            dma((2 * SIDE - 2,)),
+            dma((2 * SIDE - 2,)),
             dma((n_local * (2 * SIDE - 2),)),
             dma((n_local * (2 * SIDE - 2),)),
-            dma((n_local,)),
-            dma((n_local,)),
+            dma((n_local * (2 * SIDE - 2),)),
+            dma((n_local * (2 * SIDE - 2),)),
+            dma((2 * SIDE - 2,)),
+            dma((2 * SIDE - 2,)),
             dma((3,)),
         ],
         compiler_params=pltpu.CompilerParams(

time: 170 us -> 166 us (0.976)
  Pallas kernels: 165 us -> 160 us
    pallas_call x1, Pallas kernels: 105 us -> 100 us  [experts(): pl.pallas_call(expert_kernel, in_specs=[vmem] * 5 + [hbm] * 3, out_specs=...]
where the time goes in v7:
time: 166 us; the launch traced here: 164 us
  Pallas kernels  160 us (96%)
  local copies, waits for them, and re-layouts  3.73 us (2%)
    pallas_call x1, Pallas kernels, experts(): pl.pallas_call(expert_kernel, in_specs=[vmem] * 5 + [hbm] * 3, out_specs=...  100 us
    pallas_call x1, Pallas kernels, front(): pl.pallas_call(front_kernel, in_specs=[vmem] * 8, out_specs=[vmem] * 2, o...  60.1 us
    unnamed x2, local copies, waits for them, and re-layouts  3.73 us

profile of v7, /device:TPU:6, one launch (start us, length us, event | category | flops | bytes accessed | tf_op | source)
XLA Modules:
  0.0 164.4 jit_solution(8379872329467456796)
XLA Ops:
  0.6 60.1 %front.1 = (bf16[256,1536]{1,0:T(8,128)(2,1)}, bf16[8,256,512]{2,1,0:T(8,128)(2,1)}) custom-call(bf16[256,1536]{1,0:T(8,128)(2,1)} %tokens_ref.1, f32[1536]{0:T(1024)} %gain_ref.2, bf16[1536,256]{1,0:T(8,128)(2,1)} %weight_ref.1, bf16[1,16,1536]{2,1,0:T(8,128)(2,1)} %bitcast.8, bf16[1,16,1536]{2,1,0:T(8,128)(2,1)} %up_ref.1, s32[1,4]{1,0:T(1,128)} %lengths_ref.1, ...), custom_call_target="tpu_custom_call" | custom-call | tf_op jit(solution)/shard_map/front/pallas_call | solution.py:465
  60.7 100.0 %experts.1 = (bf16[256,1536]{1,0:T(8,128)(2,1)}, bf16[2,128,512]{2,1,0:T(8,128)(2,1)}) custom-call(bf16[256,1536]{1,0:T(8,128)(2,1)} %get-tuple-element.4.residual_ref, f32[1536]{0:T(1024)} %gain_ref.3, bf16[32,1536]{1,0:T(8,128)(2,1)} %bitcast.7, s32[4,256]{1,0:T(4,128)} %bitcast.9, s32[1,16]{1,0:T(1,128)} %page_slots_ref.1, bf16[16,128,512]{2,1,0:T(8,128)(2,1)} %bitcast.5, ...), custom_call_target="tpu_custom_call" | custom-call | tf_op jit(solution)/shard_map/experts/pallas_call | solution.py:849
  160.7 2.1 %copy.18 = bf16[256,1536]{1,0:T(8,128)(2,1)} copy(bf16[256,1536]{1,0:T(8,128)(2,1)} %get-tuple-element.8) | data formatting | bytes 1572864
  162.8 1.7 %copy.19 = bf16[2,128,512]{2,1,0:T(8,128)(2,1)} copy(bf16[2,128,512]{2,1,0:T(8,128)(2,1)} %get-tuple-element.9) | data formatting | bytes 524288

commit v8 on v7

--- a/solution.py
+++ b/solution.py
@@ -1,3 +1,5 @@
+import math
+
 import jax
 import jax.numpy as jnp
 from jax import lax
@@ -412,7 +414,7 @@
                 )
                 scores = scores + bias[...]
                 row_max = jnp.max(scores, axis=1, keepdims=True)
-                expd = jnp.exp((scores - row_max) * HEAD_SIZE ** (-0.5))
+                expd = jnp.exp2((scores - row_max) * (HEAD_SIZE ** (-0.5) * math.log2(math.e)))
                 total = jnp.sum(expd, axis=1, keepdims=True)
                 mixed = jnp.dot(
                     expd.astype(jnp.bfloat16), values, preferred_element_type=jnp.float32
@@ -689,18 +691,34 @@
         middle[0, e, 0] = produced[e, 0, :, :, :half]
         middle[1, e, 0] = produced[e, :, 0, :, half:]
 
-    def give_back(part, e, d):
+    def give_back(part, e, d, i):
         if part == 0:
-            made = produced.at[e, d, :, :, pl.ds(0, half)]
+            made = produced.at[e, d, i, :, pl.ds(0, half)]
         else:
-            made = produced.at[e, :, d, :, pl.ds(half, half)]
-        sem = (e * 2 + part) * (side - 1) + d - 1
+            made = produced.at[e, i, d, :, pl.ds(half, half)]
+        sem = (e * 2 + part) * side + i
         return pltpu.make_async_remote_copy(
             src_ref=made,
-            dst_ref=middle.at[part, e, d],
+            dst_ref=middle.at[part, e, d, i],
             send_sem=back_send.at[sem],
             recv_sem=back_recv.at[sem],
             device_id={"dp": peer_at(1 - part, side - d)},
+            device_id_type=MESH,
+        )
+
+    def given_back(part, e, i):
+        others = slice(1, side)
+        if part == 0:
+            made = produced.at[e, others, i, :, pl.ds(0, half)]
+        else:
+            made = produced.at[e, i, others, :, pl.ds(half, half)]
+        sem = (e * 2 + part) * side + i
+        return pltpu.make_async_remote_copy(
+            src_ref=made,
+            dst_ref=middle.at[part, e, others, i],
+            send_sem=back_send.at[sem],
+            recv_sem=back_recv.at[sem],
+            device_id={"dp": peer_at(1 - part, 1)},
             device_id_type=MESH,
         )
 
@@ -797,21 +815,22 @@
             for d in range(1, side):
                 legs(part, e, d).wait_recv()
         compute(e)
-        for d in (2, 1, 3):
-            for part in (0, 1):
-                give_back(part, e, d).start()
-    for e in range(n_local):
-        for d in range(1, side):
-            for part in (0, 1):
-                give_back(part, e, d).wait_recv()
+        for i in (2, 1, 3, 0):
+            for d in (2, 1, 3):
+                for part in (0, 1):
+                    give_back(part, e, d, i).start()
     ready = None
     for i in (2, 1, 3):
         for part in (0, 1):
+            for e in range(n_local):
+                given_back(part, e, i).wait_recv()
             folding[part, i] = partial(part, i).astype(jnp.bfloat16)
             if ready:
                 fold(*ready).start()
             ready = (part, i)
     for part in (0, 1):
+        for e in range(n_local):
+            given_back(part, e, 0).wait_recv()
         cols = pl.ds(part * half, half)
         total[:, cols] = residual_ref[:, cols].astype(jnp.float32) + partial(part, 0)
         if ready:
@@ -833,7 +852,9 @@
             fold(part, d).wait_send()
             for e in range(n_local):
                 legs(part, e, d).wait_send()
-                give_back(part, e, d).wait_send()
+        for e in range(n_local):
+            for i in range(side):
+                given_back(part, e, i).wait_send()
 
 
 def experts(
@@ -882,8 +903,8 @@
             dma((2 * SIDE - 2,)),
             dma((n_local * (2 * SIDE - 2),)),
             dma((n_local * (2 * SIDE - 2),)),
-            dma((n_local * (2 * SIDE - 2),)),
-            dma((n_local * (2 * SIDE - 2),)),
+            dma((n_local * 2 * SIDE,)),
+            dma((n_local * 2 * SIDE,)),
             dma((2 * SIDE - 2,)),
             dma((2 * SIDE - 2,)),
             dma((3,)),
@@ -893,6 +914,25 @@
         ),
         name="experts",
     )(residual, gain, router, routes, page_slots, group_kv, gate_up_weight, down_weight)
+
+
+def finish_kernel(layer_ref, pool_ref, layer_out_ref, pool_out_ref):
+    layer_out_ref[...] = layer_ref[...]
+    pool_out_ref[...] = pool_ref[...]
+
+
+def finish(layer_out, pool):
+    vmem = pl.BlockSpec(memory_space=pltpu.VMEM)
+    return pl.pallas_call(
+        finish_kernel,
+        in_specs=[vmem] * 2,
+        out_specs=[vmem] * 2,
+        out_shape=[
+            jax.ShapeDtypeStruct(layer_out.shape, layer_out.dtype),
+            jax.ShapeDtypeStruct(pool.shape, pool.dtype),
+        ],
+        name="finish",
+    )(layer_out, pool)
 
 
 def shards(
@@ -933,7 +973,7 @@
         expert_gate_up_weight,
         expert_down_weight,
     )
-    return (layer_out, pool)
+    return tuple(finish(layer_out, pool))
 
 
 def solution(mesh):

time: 166 us -> 160 us (0.964)
  local copies, waits for them, and re-layouts: 3.73 us -> 0 us
    unnamed x2 -> x0, local copies, waits for them, and re-layouts: 3.73 us -> none
    pallas_call x1, Pallas kernels: 100 us -> 97.1 us  [experts(): pl.pallas_call(expert_kernel, in_specs=[vmem] * 5 + [hbm] * 3, out_specs=...]
    pallas_call x0 -> x1, Pallas kernels: none -> 2.2 us  [finish(): pl.pallas_call(finish_kernel, in_specs=[vmem] * 2, out_specs=[vmem] * 2,...]
where the time goes in v8:
time: 160 us
  Pallas kernels  159 us (99%)
    pallas_call x1, Pallas kernels, experts(): pl.pallas_call(expert_kernel, in_specs=[vmem] * 5 + [hbm] * 3, out_specs=...  97.1 us
    pallas_call x1, Pallas kernels, front(): pl.pallas_call(front_kernel, in_specs=[vmem] * 8, out_specs=[vmem] * 2, o...  59.6 us

profile of v8, /device:TPU:6, one launch (start us, length us, event | category | flops | bytes accessed | tf_op | source)
XLA Modules:
  0.0 159.6 jit_solution(16928464308624665068)
XLA Ops:
  0.6 59.6 %front.1 = (bf16[256,1536]{1,0:T(8,128)(2,1)}, bf16[8,256,512]{2,1,0:T(8,128)(2,1)}) custom-call(bf16[256,1536]{1,0:T(8,128)(2,1)} %tokens_ref.1, f32[1536]{0:T(1024)} %gain_ref.2, bf16[1536,256]{1,0:T(8,128)(2,1)} %weight_ref.1, bf16[1,16,1536]{2,1,0:T(8,128)(2,1)} %bitcast.8, bf16[1,16,1536]{2,1,0:T(8,128)(2,1)} %up_ref.1, s32[1,4]{1,0:T(1,128)} %lengths_ref.1, ...), custom_call_target="tpu_custom_call" | custom-call | tf_op jit(solution)/shard_map/front/pallas_call | solution.py:467
  60.3 97.1 %experts.1 = (bf16[256,1536]{1,0:T(8,128)(2,1)}, bf16[2,128,512]{2,1,0:T(8,128)(2,1)}) custom-call(bf16[256,1536]{1,0:T(8,128)(2,1)} %get-tuple-element.6.residual_ref, f32[1536]{0:T(1024)} %gain_ref.3, bf16[32,1536]{1,0:T(8,128)(2,1)} %bitcast.7, s32[4,256]{1,0:T(4,128)} %bitcast.9, s32[1,16]{1,0:T(1,128)} %page_slots_ref.1, bf16[16,128,512]{2,1,0:T(8,128)(2,1)} %bitcast.5, ...), custom_call_target="tpu_custom_call" | custom-call | tf_op jit(solution)/shard_map/experts/pallas_call | solution.py:870
  157.4 2.2 %finish.1 = (bf16[256,1536]{1,0:T(8,128)(2,1)}, bf16[2,128,512]{2,1,0:T(8,128)(2,1)}) custom-call(bf16[256,1536]{1,0:T(8,128)(2,1)} %get-tuple-element.8.layer_ref, bf16[2,128,512]{2,1,0:T(8,128)(2,1)} %get-tuple-element.9.pool_ref), custom_call_target="tpu_custom_call" | custom-call | tf_op jit(solution)/shard_map/finish/pallas_call | solution.py:926
